TPU v7x, 256 devices: a whole 4x4x8 slice. The times are simulated.
256 devices in a mesh: gx: 16 (over z, core), gy: 4 (over x), gz: 4 (over y).
Axes of the slice: x: 4, y: 4, z: 8, core: 2. Of those that a mesh axis runs over, the one named last changes fastest.
Arguments:
- field: float32 [128, 1024, 2048], P('gz', 'gx', 'gy'), may hold values from -6 to 6
Outputs:
- coeffs: float32 [128, 1024, 2048], P('gz', 'gx', 'gy')
All inputs are finite; a program needn't handle non-finite values.
Results may differ from a plain program's by a relative error of at most 0.000075.
Values sent between devices are 32-bit elements; how exact they have to be, the bound alone decides.
A program may use at most 128 MiB of HBM per device.

v0:
```python
import functools

import jax
import jax.numpy as jnp
import numpy as np
from jax import lax
from jax.experimental import pallas as pl
from jax.experimental.pallas import tpu as pltpu
from jax.sharding import PartitionSpec as P

A = -1.586134342
B = -0.05298011854
G = 0.8829110762
E = 0.4435068522
Z = 1.149604398
MESH = pl.DeviceIdType.MESH
LANES = 128
TILES = 4
LEVELS = 3
SIDES = (0, 1)
f32, bf16 = jnp.float32, jnp.bfloat16


def filter_taps():
    u = np.eye(64)
    s, d = u[0::2].copy(), u[1::2].copy()
    d += A * (s + np.roll(s, -1, 0))
    s += B * (np.roll(d, 1, 0) + d)
    d += G * (s + np.roll(s, -1, 0))
    s += E * (np.roll(d, 1, 0) + d)
    low, high = s[16] * Z, d[16] / Z
    return [float(low[32 + o]) for o in range(5)], [float(high[33 + o]) for o in range(5)]


LOW, HIGH = filter_taps()

FROM_LEFT = {
    0: (Z * (B + E * (1 + 3 * G * B)), Z * E * G),
    1: (G * B / Z, 0.0),
    2: (Z * E * G * B, 0.0),
}
FROM_RIGHT = {
    -4: (Z * E * G * B * A, 0.0),
    -3: (G * B * A / Z, 0.0),
    -2: (Z * (B * A + E * (G * B * A + A * (1 + 2 * G * B))), Z * E * G),
    -1: (A * (1 + 2 * G * B) / Z, G / Z),
}


def tap_weights(position, target, step):
    apart = jnp.abs(position - target)
    phase = target % (2 * step)
    low = jnp.zeros(position.shape, f32)
    high = jnp.zeros(position.shape, f32)
    for o in range(5):
        low = jnp.where(apart == o * step, LOW[o], low)
        if o < 4:
            high = jnp.where(apart == o * step, HIGH[o], high)
    rest = jnp.where(apart == 0, 1.0, 0.0) if step > 1 else high
    return jnp.where(phase == 0, low, jnp.where(phase == step, high, rest))


def parts_of(values):
    top = values.astype(bf16)
    return top, (values - top.astype(f32)).astype(bf16)


def encode_end(s2, d2, s1, d1):
    return d1 + A * s1, s1 + B * (d2 + A * (s2 + s1))


def encode_start(s0, d0, s1):
    return s0, s0 + B * (d0 + A * (s0 + s1))


def lift_list(u, halo=None):
    s, d = list(u[0::2]), list(u[1::2])
    count = len(s)
    d_before = A * s[0]
    if halo is not None:
        d_before = d_before + halo[0]
    s_before = B * d_before
    if halo is not None:
        s_before = s_before + halo[1]
    for i in range(count - 1):
        d[i] = d[i] + A * (s[i] + s[i + 1])
    last = s[-1] if halo is None else s[-1] + halo[2]
    d[-1] = d[-1] + A * last
    s_after = B * d[-1]
    if halo is not None:
        s_after = s_after + halo[3]
    around = [d_before] + d
    s = [s[i] + B * (around[i] + around[i + 1]) for i in range(count)]
    d_before = d_before + G * (s_before + s[0])
    around = s + [s_after]
    d = [d[i] + G * (around[i] + around[i + 1]) for i in range(count)]
    around = [d_before] + d
    s = [s[i] + E * (around[i] + around[i + 1]) for i in range(count)]
    out = []
    for i in range(count):
        out += [s[i] * Z, d[i] * (1.0 / Z)]
    return out


def lift_rows(flat, start, height):
    half = height // 2
    pair = lax.broadcasted_iota(jnp.int32, (half, LANES), 0)
    even, odd = pl.ds(start, half, stride=2), pl.ds(start + 1, half, stride=2)
    s, d = flat[even, :], flat[odd, :]

    def after(values, last):
        return jnp.where(pair == half - 1, last, pltpu.roll(values, half - 1, 0))

    def before(values, first):
        return jnp.where(pair == 0, first, pltpu.roll(values, 1, 0))

    d_before = A * s[:1]
    d = d + A * (s + after(s, 0.0))
    s_after = B * d[half - 1 :]
    s_before = B * d_before
    s = s + B * (before(d, d_before) + d)
    d_before = d_before + G * (s_before + s[:1])
    d = d + G * (s + after(s, s_after))
    s = s + E * (before(d, d_before) + d)
    flat[even, :] = s * Z
    flat[odd, :] = d * (1.0 / Z)


def lift_lanes(tiles, ext, weights):
    first = lax.broadcasted_iota(jnp.int32, tiles[0].shape, 1) < LANES // 2
    out = []
    for block in range(2):
        main = jnp.concatenate([tiles[2 * block], tiles[2 * block + 1]], axis=1)
        beside = jnp.where(first, tiles[2], ext) if block == 0 else jnp.where(first, ext, tiles[1])
        main_top, main_low = parts_of(main)
        side_top, side_low = parts_of(beside)
        stacked = jnp.concatenate([main_top, main_low, main_top, side_top, side_low, side_top], axis=1)
        result = jnp.dot(stacked, weights[...], preferred_element_type=f32)
        out += [result[:, :LANES], result[:, LANES:]]
    return out


def sizes_of(shape, level):
    return shape[0] >> level, shape[1] >> level


def kernel(shape, field_ref, out_ref, *scratch):
    depth, rows, _ = shape
    refs = list(scratch)
    take = lambda: refs.pop(0)
    bodies = [out_ref, take(), take()]
    load_sem, send_sem, recv_sem = take(), take(), take()
    y_weights, far_weights, z_weights = [[take() for _ in range(LEVELS)] for _ in range(3)]
    per_level = [{} for _ in range(LEVELS)]
    for level in range(LEVELS):
        for name in ("zs", "zr", "ze", "xs", "xr", "xe", "xl", "es", "er", "ys", "yr", "zys", "zyr", "xys", "xyr", "cr"):
            per_level[level][name] = take()

    here = {name: lax.axis_index(name) for name in ("gx", "gy", "gz")}
    count = {name: lax.axis_size(name) for name in ("gx", "gy", "gz")}

    def beside(**by):
        return {name: lax.rem(here[name] + way + count[name], count[name]) for name, way in by.items()}

    loads = [
        pltpu.make_async_copy(
            field_ref.at[:, :, pl.ds(tile * LANES, LANES)], out_ref.at[:, tile], load_sem.at[tile]
        )
        for tile in range(TILES)
    ]
    for load in loads:
        load.start()

    barrier = pltpu.get_barrier_semaphore()
    for x in (-1, 0, 1):
        for y in (-1, 0, 1):
            for z in (-1, 0, 1):
                if (x, y, z) != (0, 0, 0):
                    pl.semaphore_signal(barrier, inc=1, device_id=beside(gx=x, gy=y, gz=z), device_id_type=MESH)

    def make_weights(level):
        step = 2**level
        window = 4 * step
        row = lax.broadcasted_iota(jnp.int32, (2 * LANES, 2 * LANES), 0)
        col = lax.broadcasted_iota(jnp.int32, (2 * LANES, 2 * LANES), 1)
        near, low = parts_of(tap_weights(row, col, step))
        weights = y_weights[level]
        weights[0 : 2 * LANES] = near
        weights[2 * LANES : 4 * LANES] = near
        weights[4 * LANES : 6 * LANES] = low
        side = row[:LANES]
        position = jnp.where(side < LANES // 2, 2 * LANES + side, side - LANES)
        near, low = parts_of(tap_weights(position, col[:LANES], step))
        weights[6 * LANES : 7 * LANES] = near
        weights[7 * LANES : 8 * LANES] = near
        weights[8 * LANES : 9 * LANES] = low
        left = row < LANES
        position = jnp.where(left, row % window - window, LANES + row % window)
        taps = tap_weights(position, col % LANES, step)
        near, low = parts_of(jnp.where(left == (col < LANES), taps, 0.0))
        weights = far_weights[level]
        weights[0 : 2 * LANES] = near
        weights[2 * LANES : 4 * LANES] = near
        weights[4 * LANES : 6 * LANES] = low
        row, col = row[:LANES, :LANES], col[:LANES, :LANES]
        taps = tap_weights(row // window, col // window, 1)
        near, low = parts_of(jnp.where(row % window == col % window, taps, 0.0))
        weights = z_weights[level]
        weights[0:LANES] = near
        weights[LANES : 2 * LANES] = near
        weights[2 * LANES : 3 * LANES] = low

    make_weights(0)
    for load in loads:
        load.wait()

    sends = []
    sub = lax.broadcasted_iota(jnp.int32, (8, LANES), 0)
    lane8 = lax.broadcasted_iota(jnp.int32, (8, LANES), 1)

    def per_row(table, layer):
        values = jnp.zeros((8, LANES), f32)
        for number, weights in table.items():
            if weights[layer] != 0.0:
                values = jnp.where(sub == number % 8, weights[layer], values)
        return values

    for level in range(LEVELS):
        step = 2**level
        window = 4 * step
        planes, height = depth // step, rows // step
        body = bodies[level]
        flat = body.reshape(planes * TILES * height, LANES)
        r = per_level[level]
        arrivals = {}

        def send(key, number, source, target, **by):
            copy = pltpu.make_async_remote_copy(
                src_ref=source,
                dst_ref=target,
                send_sem=send_sem.at[level, number],
                recv_sem=recv_sem.at[level, number],
                device_id=beside(**by),
                device_id_type=MESH,
            )
            if level == 0 and number == 0:
                pl.semaphore_wait(barrier, 26)
            copy.start()
            sends.append(copy)
            arrivals.setdefault(key, []).append(copy)

        way = (1, -1)
        zs, xs, es = r["zs"], r["xs"], r["es"]
        def encode_z(tile, _):
            end = encode_end(*[body[planes - 4 + number, tile] for number in range(4)])
            start = encode_start(*[body[number, tile] for number in range(3)])
            for k in range(2):
                zs[0, k, tile] = end[k]
                zs[1, k, tile] = start[k]
            return 0

        lax.fori_loop(0, TILES, encode_z, 0)
        for side in SIDES:
            send("z", side, zs.at[side], r["zr"].at[side], gz=way[side])

        xs_flat = xs.reshape(2 * planes * 8, LANES)
        for tile in range(TILES):
            def at(number):
                return flat[pl.ds(tile * height + number, planes, stride=TILES * height), :]

            end = encode_end(*[at(height - 4 + number) for number in range(4)])
            start = encode_start(*[at(number) for number in range(3)])
            for k in range(2):
                xs_flat[pl.ds(k * TILES + tile, planes, stride=8), :] = end[k]
                xs_flat[pl.ds(planes * 8 + k * TILES + tile, planes, stride=8), :] = start[k]
        for side in SIDES:
            send("x", 2 + side, xs.at[side], r["xr"].at[side], gx=way[side])

        for side in SIDES:
            end = encode_end(*[xs[side, planes - 4 + number] for number in range(4)])
            start = encode_start(*[xs[side, number] for number in range(3)])
            for k in range(2):
                es[side, 0, k] = end[k]
                es[side, 1, k] = start[k]
        for sx in SIDES:
            for sz in SIDES:
                send("e", 4 + 2 * sx + sz, es.at[sx, sz], r["er"].at[sx, sz], gx=way[sx], gz=way[sz])
                for sy in SIDES:
                    send(
                        "c",
                        8 + 4 * sx + 2 * sz + sy,
                        es.at[sx, sz],
                        r["cr"].at[sx, sz, sy],
                        gx=way[sx],
                        gz=way[sz],
                        gy=way[sy],
                    )

        lane = lax.broadcasted_iota(jnp.int32, (height, LANES), 1)

        def pack(plane, held):
            to_right, to_left, x_right, x_left = held
            tail_by = lax.rem(plane * window + window, LANES)
            head_by = plane * window
            mine = lane // window == plane
            to_right = jnp.where(mine, pltpu.roll(body[plane, TILES - 1], tail_by, 1), to_right)
            to_left = jnp.where(mine, pltpu.roll(body[plane, 0], head_by, 1), to_left)
            mine = lane8 // window == plane
            x_right = tuple(jnp.where(mine, pltpu.roll(xs[sx, plane], tail_by, 1), x_right[sx]) for sx in SIDES)
            x_left = tuple(jnp.where(mine, pltpu.roll(xs[sx, plane], head_by, 1), x_left[sx]) for sx in SIDES)
            return to_right, to_left, x_right, x_left

        none = jnp.zeros((height, LANES), f32)
        none8 = jnp.zeros((8, LANES), f32)
        to_right, to_left, x_right, x_left = lax.fori_loop(
            0, planes, pack, (none, none, (none8, none8), (none8, none8))
        )
        r["ys"][0], r["ys"][1] = to_right, to_left
        for sx in SIDES:
            r["xys"][0, sx], r["xys"][1, sx] = x_right[sx], x_left[sx]
        groups = height // 8
        for sz in SIDES:
            tail = head = none8
            for k in range(2):
                for group in range(groups):
                    slot = k * groups + group
                    mine = lane8 // window == slot
                    part = pl.ds(group * 8, 8)
                    by = (slot * window + window) % LANES
                    tail = jnp.where(mine, pltpu.roll(zs[sz, k, TILES - 1, part, :], by, 1), tail)
                    head = jnp.where(mine, pltpu.roll(zs[sz, k, 0, part, :], slot * window, 1), head)
            r["zys"][0, sz], r["zys"][1, sz] = tail, head
        for sy in SIDES:
            send("y", 16 + sy, r["ys"].at[sy], r["yr"].at[sy], gy=way[sy])
            for s in SIDES:
                send("xy", 18 + 2 * sy + s, r["xys"].at[sy, s], r["xyr"].at[sy, s], gy=way[sy], gx=way[s])
                send("zy", 22 + 2 * sy + s, r["zys"].at[sy, s], r["zyr"].at[sy, s], gy=way[sy], gz=way[s])

        if level == 0:
            for other in range(1, LEVELS):
                make_weights(other)

        def own_x(plane, _):
            for tile in range(TILES):
                lift_rows(flat, (plane * TILES + tile) * height, height)
            return 0

        lax.fori_loop(0, planes, own_x, 0)

        def own_z(block, _):
            tile = block // groups
            part = pl.ds(pl.multiple_of((block % groups) * 8, 8), 8)
            lifted = lift_list([body[plane, tile, part, :] for plane in range(planes)])
            for plane in range(planes):
                body[plane, tile, part, :] = lifted[plane]
            return 0

        lax.fori_loop(0, TILES * groups, own_z, 0)

        chunk = min(planes, 512 // height)
        weights = y_weights[level]

        def own_y(number, _):
            where = pl.ds(number * chunk, chunk)
            tiles = [body[where, tile].reshape(chunk * height, LANES) for tile in range(TILES)]
            lifted = lift_lanes(tiles, jnp.zeros((chunk * height, LANES), f32), weights)
            for tile in range(TILES):
                body[where, tile] = lifted[tile].reshape(chunk, height, LANES)
            return 0

        lax.fori_loop(0, planes // chunk, own_y, 0)

        for copy in arrivals["y"]:
            copy.wait_recv()
        packed = []
        for sy in SIDES:
            held = r["yr"].at[sy]
            lift_rows(held, 0, height)
            top, low = parts_of(held[...])
            stacked = jnp.concatenate([top, low, top], axis=1)
            packed.append(jnp.dot(stacked, z_weights[level][...], preferred_element_type=f32))
        packed = [part for values in packed for part in (values,)]
        tops = [values.astype(bf16).astype(f32) for values in packed]
        lows = [values - top for values, top in zip(packed, tops)]
        far = far_weights[level]
        r["ys"]

        def far_y(number, _):
            stacks = []
            for inner in range(chunk):
                mine = lane // window == number * chunk + inner
                top = [jnp.where(mine, values, 0.0).astype(bf16) for values in tops]
                low = [jnp.where(mine, values, 0.0).astype(bf16) for values in lows]
                stacks.append(jnp.concatenate(top + low + top, axis=1))
            added = jnp.dot(jnp.concatenate(stacks, axis=0), far[...], preferred_element_type=f32)
            where = pl.ds(number * chunk, chunk)
            body[where, 0] = body[where, 0] + added[:, :LANES].reshape(chunk, height, LANES)
            body[where, TILES - 1] = body[where, TILES - 1] + added[:, LANES:].reshape(chunk, height, LANES)
            return 0

        lax.fori_loop(0, planes // chunk, far_y, 0)

        for key in ("x", "e", "c", "xy"):
            for copy in arrivals[key]:
                copy.wait_recv()
        xr, xe, xl = r["xr"], r["xe"], r["xl"]
        last_half = lane8 >= LANES // 2

        def unpack_x(plane, _):
            left_by = lax.rem(2 * LANES - window - plane * window, LANES)
            right_by = lax.rem(LANES - plane * window, LANES)
            for sx in SIDES:
                left = pltpu.roll(pltpu.roll(r["xyr"][0, sx], 5, 0), left_by, 1)
                right = pltpu.roll(r["xyr"][1, sx], right_by, 1)
                xe[sx, plane] = jnp.where(last_half, left, right)
            return 0

        lax.fori_loop(0, planes, unpack_x, 0)
        for sx in SIDES:
            halo = [r["er"][sx, sz, k] for sz in SIDES for k in range(2)]
            lifted = lift_list([xr[sx, plane] for plane in range(planes)], halo)
            for plane in range(planes):
                xr[sx, plane] = lifted[plane]
            halo = [
                jnp.where(last_half, pltpu.roll(r["cr"][sx, sz, 0, k], 5, 0), r["cr"][sx, sz, 1, k])
                for sz in SIDES
                for k in range(2)
            ]
            lifted = lift_list([xe[sx, plane] for plane in range(planes)], halo)
            for plane in range(planes):
                xe[sx, plane] = lifted[plane]
        xr_flat = xr.reshape(2 * planes * 8, LANES)
        xe_flat = xe.reshape(2 * planes * 8, LANES)
        for k in range(2):
            tiles = [xr_flat[pl.ds(k * TILES + tile, 2 * planes, stride=8), :] for tile in range(TILES)]
            ext = xe_flat[pl.ds(k * TILES, 2 * planes, stride=8), :]
            lifted = lift_lanes(tiles, ext, weights)
            for tile in range(TILES):
                xl[k, tile] = lifted[tile]
        left_rows = [per_row(FROM_LEFT, layer) for layer in range(2)]
        right_rows = [per_row(FROM_RIGHT, layer) for layer in range(2)]

        def far_x(plane, _):
            for tile in range(TILES):
                for side, weigh, top in ((0, left_rows, 0), (1, right_rows, height - 8)):
                    part = pl.ds(top, 8)
                    at = pl.ds(side * planes + plane, 1)
                    added = weigh[0] * xl[0, tile, at, :] + weigh[1] * xl[1, tile, at, :]
                    body[plane, tile, part, :] = body[plane, tile, part, :] + added
            return 0

        lax.fori_loop(0, planes, far_x, 0)

        for key in ("zy", "z"):
            for copy in arrivals[key]:
                copy.wait_recv()
        zr, ze = r["zr"], r["ze"]
        zr_flat = zr.reshape(4 * TILES * height, LANES)
        ze_flat = ze.reshape(4 * height, LANES)
        for sz in SIDES:
            for k in range(2):
                for group in range(groups):
                    slot = k * groups + group
                    left = pltpu.roll(r["zyr"][0, sz], (2 * LANES - window - slot * window) % LANES, 1)
                    right = pltpu.roll(r["zyr"][1, sz], (LANES - slot * window) % LANES, 1)
                    ze[sz, k, pl.ds(group * 8, 8), :] = jnp.where(last_half, left, right)

        def far_z_rows(layer, _):
            for tile in range(TILES):
                lift_rows(zr_flat, (layer * TILES + tile) * height, height)
            lift_rows(ze_flat, layer * height, height)
            return 0

        lax.fori_loop(0, 4, far_z_rows, 0)
        tiles = [zr[:, :, tile].reshape(4 * height, LANES) for tile in range(TILES)]
        lifted = lift_lanes(tiles, ze[...].reshape(4 * height, LANES), weights)
        for tile in range(TILES):
            layers = [lifted[tile][k * height : (k + 1) * height] for k in range(4)]
            for first, table in ((0, FROM_LEFT), (2, FROM_RIGHT)):
                for number, (one, two) in table.items():
                    plane = number % planes
                    added = one * layers[first]
                    if two != 0.0:
                        added = added + two * layers[first + 1]
                    body[plane, tile] = body[plane, tile] + added

        if level < LEVELS - 1:
            inner = bodies[level + 1]

            def pick(plane, _):
                for tile in range(TILES):
                    start = (2 * plane * TILES + tile) * height
                    inner[plane, tile] = flat[pl.ds(start, height // 2, stride=2), :]
                return 0

            lax.fori_loop(0, planes // 2, pick, 0)

    for level in (1, 0):
        step = 2**level
        planes, height = depth // step, rows // step
        half = height // 2
        inner = bodies[level + 1]
        flat = bodies[level].reshape(planes * TILES * height, LANES)
        keep = lax.broadcasted_iota(jnp.int32, (half, LANES), 1) % (2 * step) == 0

        def place(plane, _):
            for tile in range(TILES):
                start = (2 * plane * TILES + tile) * height
                where = pl.ds(start, half, stride=2)
                flat[where, :] = jnp.where(keep, inner[plane, tile], flat[where, :])
            return 0

        lax.fori_loop(0, planes // 2, place, 0)

    for copy in sends:
        copy.wait_send()


def write_out(held_ref, out_ref, sem):
    copies = [
        pltpu.make_async_copy(held_ref.at[:, tile], out_ref.at[:, :, pl.ds(tile * LANES, LANES)], sem.at[tile])
        for tile in range(TILES)
    ]
    for copy in copies:
        copy.start()
    for copy in copies:
        copy.wait()


def local(field):
    depth, rows, lanes = field.shape
    vmem = pltpu.VMEM
    sizes = [(depth >> level, rows >> level) for level in range(LEVELS)]
    scratch = [vmem((planes, TILES, height, LANES), f32) for planes, height in sizes[1:]]
    scratch += [
        pltpu.SemaphoreType.DMA((TILES,)),
        pltpu.SemaphoreType.DMA((LEVELS, 26)),
        pltpu.SemaphoreType.DMA((LEVELS, 26)),
    ]
    for shape in ((9 * LANES, 2 * LANES), (6 * LANES, 2 * LANES), (3 * LANES, LANES)):
        scratch += [vmem(shape, bf16)] * LEVELS
    for planes, height in sizes:
        shapes = [(2, 2, TILES, height)] * 2 + [(2, 2, height)]
        shapes += [(2, planes, 8)] * 3 + [(2, TILES, 2 * planes)]
        shapes += [(2, 2, 2, 8)] * 2 + [(2, height)] * 2 + [(2, 2, 8)] * 4 + [(2, 2, 2, 2, 8)]
        scratch += [vmem((*shape, LANES), f32) for shape in shapes]
    held = pl.pallas_call(
        functools.partial(kernel, field.shape),
        out_shape=jax.ShapeDtypeStruct((depth, TILES, rows, LANES), f32),
        in_specs=[pl.BlockSpec(memory_space=pltpu.HBM)],
        out_specs=pl.BlockSpec(memory_space=pltpu.VMEM),
        scratch_shapes=scratch,
        compiler_params=pltpu.CompilerParams(
            collective_id=0, has_side_effects=True, vmem_limit_bytes=40 * 2**20
        ),
        name="lift",
    )(field)
    return pl.pallas_call(
        write_out,
        out_shape=jax.ShapeDtypeStruct(field.shape, f32),
        in_specs=[pl.BlockSpec(memory_space=pltpu.VMEM)],
        out_specs=pl.BlockSpec(memory_space=pltpu.HBM),
        scratch_shapes=[pltpu.SemaphoreType.DMA((TILES,))],
        compiler_params=pltpu.CompilerParams(vmem_limit_bytes=8 * 2**20),
        name="write_out",
    )(held)


def solution(mesh):
    placed = (P("gz", "gx", "gy"),)
    return jax.shard_map(
        local, mesh=mesh, in_specs=placed, out_specs=P("gz", "gx", "gy"), check_vma=False
    )
```

profile of v0, /device:TPU:1, one launch (start us, length us, event | category | flops | bytes accessed | tf_op | source)
XLA Modules:
  0.0 49.8 jit_solution(976725221645497027)
XLA Ops:
  0.0 0.0 copy-start
  0.0 2.2 %copy-done = f32[32,64,512]{2,1,0:T(8,128)S(1)} copy-done((f32[32,64,512]{2,1,0:T(8,128)S(1)}, f32[32,64,512]{2,1,0:T(8,128)}, u32[]{:S(2)}) %copy-start) | copy-done | bytes 4194328
  2.2 45.5 %lift.1.held_ref = f32[32,4,64,128]{3,2,1,0:T(8,128)S(1)} custom-call(f32[32,64,512]{2,1,0:T(8,128)S(1)} %copy-done), custom_call_target="tpu_custom_call" | custom-call | tf_op jit(solution)/shard_map/lift/pallas_call | solution.py:547
  47.7 2.0 %write_out.1 = f32[32,64,512]{2,1,0:T(8,128)} custom-call(f32[32,4,64,128]{3,2,1,0:T(8,128)S(1)} %lift.1.held_ref), custom_call_target="tpu_custom_call" | custom-call | tf_op jit(solution)/shard_map/write_out/pallas_call | solution.py:558
Async XLA Ops:
  0.0 2.2 %copy-start = (f32[32,64,512]{2,1,0:T(8,128)S(1)}, f32[32,64,512]{2,1,0:T(8,128)}, u32[]{:S(2)}) copy-start(f32[32,64,512]{2,1,0:T(8,128)} %field_ref.1) | copy-start | bytes 12582916
where the time goes:
time: 49.9 us; the launch traced here: 49.8 us
  Pallas kernels  47.6 us (95%)
  local copies, waits for them, and re-layouts  2.19 us (4%)
    pallas_call x1, Pallas kernels, local(): pl.pallas_call(functools.partial(kernel, field.shape), out_shape=jax.Shap...  45.5 us
    unnamed x2, local copies, waits for them, and re-layouts  2.19 us
    pallas_call x1, Pallas kernels, local(): pl.pallas_call(write_out, out_shape=jax.ShapeDtypeStruct(field.shape, f32...  2.04 us

commit v1 on v0

v1 whole, which is shorter than its diff:
```python
import functools

import jax
import jax.numpy as jnp
import numpy as np
from jax import lax
from jax.experimental import pallas as pl
from jax.experimental.pallas import tpu as pltpu
from jax.sharding import PartitionSpec as P

A = -1.586134342
B = -0.05298011854
G = 0.8829110762
E = 0.4435068522
Z = 1.149604398
MESH = pl.DeviceIdType.MESH
LANES = 128
TILES = 4
LEVELS = 3
SIDES = (0, 1)
f32, bf16 = jnp.float32, jnp.bfloat16


def filter_taps():
    u = np.eye(64)
    s, d = u[0::2].copy(), u[1::2].copy()
    d += A * (s + np.roll(s, -1, 0))
    s += B * (np.roll(d, 1, 0) + d)
    d += G * (s + np.roll(s, -1, 0))
    s += E * (np.roll(d, 1, 0) + d)
    low, high = s[16] * Z, d[16] / Z
    return [float(low[32 + o]) for o in range(5)], [float(high[33 + o]) for o in range(5)]


LOW, HIGH = filter_taps()

FROM_LEFT = {
    0: (Z * (B + E * (1 + 3 * G * B)), Z * E * G),
    1: (G * B / Z, 0.0),
    2: (Z * E * G * B, 0.0),
}
FROM_RIGHT = {
    -4: (Z * E * G * B * A, 0.0),
    -3: (G * B * A / Z, 0.0),
    -2: (Z * (B * A + E * (G * B * A + A * (1 + 2 * G * B))), Z * E * G),
    -1: (A * (1 + 2 * G * B) / Z, G / Z),
}


def cell_of(level, tile, lane):
    if level == 0:
        return tile * LANES + lane
    if level == 1:
        turn = lane & 1
        return ((tile + 2 * turn) * LANES + lane - turn) >> 1
    turn = lane & 3
    return (((turn >> 1) + 2 * (turn & 1)) * LANES + lane - turn) >> 2


def tap_weights(position, target):
    apart = jnp.abs(position - target)
    low = jnp.zeros(position.shape, f32)
    high = jnp.zeros(position.shape, f32)
    for o in range(5):
        low = jnp.where(apart == o, LOW[o], low)
        if o < 4:
            high = jnp.where(apart == o, HIGH[o], high)
    return jnp.where((target & 1) == 0, low, high)


def parts_of(values):
    top = values.astype(bf16)
    return top, (values - top.astype(f32)).astype(bf16)


def encode_end(s2, d2, s1, d1):
    return d1 + A * s1, s1 + B * (d2 + A * (s2 + s1))


def encode_start(s0, d0, s1):
    return s0, s0 + B * (d0 + A * (s0 + s1))


def lift_list(u, halo=None):
    s, d = list(u[0::2]), list(u[1::2])
    count = len(s)
    d_before = A * s[0]
    if halo is not None:
        d_before = d_before + halo[0]
    s_before = B * d_before
    if halo is not None:
        s_before = s_before + halo[1]
    for i in range(count - 1):
        d[i] = d[i] + A * (s[i] + s[i + 1])
    last = s[-1] if halo is None else s[-1] + halo[2]
    d[-1] = d[-1] + A * last
    s_after = B * d[-1]
    if halo is not None:
        s_after = s_after + halo[3]
    around = [d_before] + d
    s = [s[i] + B * (around[i] + around[i + 1]) for i in range(count)]
    d_before = d_before + G * (s_before + s[0])
    around = s + [s_after]
    d = [d[i] + G * (around[i] + around[i + 1]) for i in range(count)]
    around = [d_before] + d
    s = [s[i] + E * (around[i] + around[i + 1]) for i in range(count)]
    out = []
    for i in range(count):
        out += [s[i] * Z, d[i] * (1.0 / Z)]
    return out


def lift_rows(flat, start, height):
    half = height // 2
    pair = lax.broadcasted_iota(jnp.int32, (half, LANES), 0)
    even, odd = pl.ds(start, half, stride=2), pl.ds(start + 1, half, stride=2)
    s, d = flat[even, :], flat[odd, :]

    def after(values, last):
        return jnp.where(pair == half - 1, last, pltpu.roll(values, half - 1, 0))

    def before(values, first):
        return jnp.where(pair == 0, first, pltpu.roll(values, 1, 0))

    d_before = A * s[:1]
    d = d + A * (s + after(s, 0.0))
    s_after = B * d[half - 1 :]
    s_before = B * d_before
    s = s + B * (before(d, d_before) + d)
    d_before = d_before + G * (s_before + s[:1])
    d = d + G * (s + after(s, s_after))
    s = s + E * (before(d, d_before) + d)
    flat[even, :] = s * Z
    flat[odd, :] = d * (1.0 / Z)


def pack_tiles(level, tiles):
    lane = lax.broadcasted_iota(jnp.int32, tiles[0].shape, 1)
    step = 2**level
    keep = lane & (2 * step - 1) < step
    half = len(tiles) // 2
    return [jnp.where(keep, tiles[i], pltpu.roll(tiles[i + half], step, 1)) for i in range(half)]


def unpack_tiles(level, tiles, inner):
    lane = lax.broadcasted_iota(jnp.int32, tiles[0].shape, 1)
    step = 2**level
    keep = lane & (2 * step - 1) < step
    inner = list(inner) + [pltpu.roll(tile, LANES - step, 1) for tile in inner]
    return [jnp.where(keep, new, old) for new, old in zip(inner, tiles)]


def lift_lanes(tiles, ext, weights):
    first = lax.broadcasted_iota(jnp.int32, tiles[0].shape, 1) < LANES // 2
    blocks = [(tiles, ext)]
    if len(tiles) == 4:
        blocks = [(tiles[:2], jnp.where(first, tiles[2], ext)), (tiles[2:], jnp.where(first, ext, tiles[1]))]
    out = []
    for main, beside in blocks:
        main_top, main_low = parts_of(jnp.concatenate(main, axis=1))
        side_top, side_low = parts_of(beside)
        stacked = jnp.concatenate([main_top, main_low, main_top, side_top, side_low, side_top], axis=1)
        result = jnp.dot(stacked, weights[...], preferred_element_type=f32)
        out += [result[:, i * LANES : (i + 1) * LANES] for i in range(len(main))]
    return out


NAMES = ("zs", "zr", "ze", "xs", "xr", "xe", "xl", "es", "er", "ys", "yr", "yp", "zys", "zyr", "xys", "xyr", "cr")


def kernel(shape, field_ref, out_ref, *scratch):
    depth, rows, _ = shape
    refs = list(scratch)
    take = lambda: refs.pop(0)
    bodies = [out_ref, take(), take()]
    load_sem, send_sem, recv_sem = take(), take(), take()
    y_weights, far_weights, z_weights = [[take() for _ in range(LEVELS)] for _ in range(3)]
    held = [{name: take() for name in NAMES} for _ in range(LEVELS)]

    here = {name: lax.axis_index(name) for name in ("gx", "gy", "gz")}
    count = {name: lax.axis_size(name) for name in ("gx", "gy", "gz")}

    def beside(**by):
        return {name: lax.rem(here[name] + way + count[name], count[name]) for name, way in by.items()}

    barrier = pltpu.get_barrier_semaphore()
    for x in (-1, 0, 1):
        for y in (-1, 0, 1):
            for z in (-1, 0, 1):
                if (x, y, z) != (0, 0, 0):
                    pl.semaphore_signal(barrier, inc=1, device_id=beside(gx=x, gy=y, gz=z), device_id_type=MESH)

    loads = [
        pltpu.make_async_copy(
            field_ref.at[:, :, pl.ds(tile * LANES, LANES)], out_ref.at[:, tile], load_sem.at[tile]
        )
        for tile in range(TILES)
    ]
    for load in loads:
        load.start()

    def fill(ref, blocks):
        start = 0
        for values in blocks:
            top, low = parts_of(values)
            size = values.shape[0]
            for part in (top, top, low):
                ref[start : start + size] = part
                start += size

    def make_weights(level):
        window = 4 << level
        tiles = TILES >> level
        cells = (TILES * LANES) >> level
        width = min(tiles, 2) * LANES
        row = lax.broadcasted_iota(jnp.int32, (2 * LANES, width), 0)
        col = lax.broadcasted_iota(jnp.int32, (2 * LANES, width), 1)
        target = cell_of(level, col >> 7, col & 127)
        main = row[:width]
        side = row[:LANES]
        after, before = (2 * LANES, -LANES) if level == 0 else (cells, -cells)
        right = cell_of(level, 0, side) + after
        left = cell_of(level, 0 if level == 0 else tiles - 1, side) + before
        position = jnp.where(side < LANES // 2, right, left)
        fill(
            y_weights[level],
            [
                tap_weights(cell_of(level, main >> 7, main & 127), target[:width]),
                tap_weights(position, target[:LANES]),
            ],
        )
        inside = row & (window - 1)
        left = cell_of(level, tiles - 1, LANES - window + inside) - cells
        right = cell_of(level, 0, inside) + cells
        position = jnp.where(row < LANES, left, right)
        last = cell_of(level, tiles - 1, col & 127)
        target = jnp.where(col < LANES, cell_of(level, 0, col & 127), last)
        fill(far_weights[level], [tap_weights(position, target)])
        shift = 2 + level
        row, col = row[:LANES, :LANES], col[:LANES, :LANES]
        taps = tap_weights(row >> shift, col >> shift)
        fill(z_weights[level], [jnp.where((row & (window - 1)) == (col & (window - 1)), taps, 0.0)])

    make_weights(0)
    for load in loads:
        load.wait()

    sends = []
    arrivals = [{} for _ in range(LEVELS)]
    way = (1, -1)
    sub = lax.broadcasted_iota(jnp.int32, (8, LANES), 0)
    lane8 = lax.broadcasted_iota(jnp.int32, (8, LANES), 1)
    last_half = lane8 >= LANES // 2
    none8 = jnp.zeros((8, LANES), f32)

    def extent(level):
        return depth >> level, TILES >> level, rows >> level, 4 << level

    def flat_of(ref):
        size = 1
        for extent_of_dim in ref.shape[:-1]:
            size *= extent_of_dim
        return ref.reshape(size, LANES)

    def wait_for(level, *keys):
        for key in keys:
            for copy in arrivals[level][key]:
                copy.wait_recv()

    def start(level):
        planes, tiles, height, window = extent(level)
        body, flat, r = bodies[level], flat_of(bodies[level]), held[level]
        shift = 2 + level

        def send(key, number, source, target, **by):
            copy = pltpu.make_async_remote_copy(
                src_ref=source,
                dst_ref=target,
                send_sem=send_sem.at[level, number],
                recv_sem=recv_sem.at[level, number],
                device_id=beside(**by),
                device_id_type=MESH,
            )
            if level == 0 and number == 0:
                pl.semaphore_wait(barrier, 26)
            copy.start()
            sends.append(copy)
            arrivals[level].setdefault(key, []).append(copy)

        zs, xs, es = r["zs"], r["xs"], r["es"]
        for tile in range(tiles):
            end = encode_end(*[body[planes - 4 + number, tile] for number in range(4)])
            begin = encode_start(*[body[number, tile] for number in range(3)])
            for k in range(2):
                zs[0, k, tile] = end[k]
                zs[1, k, tile] = begin[k]
        for side in SIDES:
            send("z", side, zs.at[side], r["zr"].at[side], gz=way[side])

        xs_flat = flat_of(xs)
        for tile in range(tiles):
            def at(number):
                return flat[pl.ds(tile * height + number, planes, stride=tiles * height), :]

            end = encode_end(*[at(height - 4 + number) for number in range(4)])
            begin = encode_start(*[at(number) for number in range(3)])
            for k in range(2):
                xs_flat[pl.ds(k * tiles + tile, planes, stride=8), :] = end[k]
                xs_flat[pl.ds(planes * 8 + k * tiles + tile, planes, stride=8), :] = begin[k]
        for side in SIDES:
            send("x", 2 + side, xs.at[side], r["xr"].at[side], gx=way[side])

        for side in SIDES:
            end = encode_end(*[xs[side, planes - 4 + number] for number in range(4)])
            begin = encode_start(*[xs[side, number] for number in range(3)])
            for k in range(2):
                es[side, 0, k] = end[k]
                es[side, 1, k] = begin[k]
        for sx in SIDES:
            for sz in SIDES:
                number = 4 + 2 * sx + sz
                send("e", number, es.at[sx, sz], r["er"].at[sx, sz], gx=way[sx], gz=way[sz])
                for sy in SIDES:
                    number = 8 + 4 * sx + 2 * sz + sy
                    send("c", number, es.at[sx, sz], r["cr"].at[sx, sz, sy], gx=way[sx], gz=way[sz], gy=way[sy])

        lane = lax.broadcasted_iota(jnp.int32, (height, LANES), 1)

        def pack(plane, carried):
            to_right, to_left, x_right, x_left = carried
            tail_by = lax.rem(plane * window + window, LANES)
            head_by = plane * window
            mine = lane >> shift == plane
            to_right = jnp.where(mine, pltpu.roll(body[plane, tiles - 1], tail_by, 1), to_right)
            to_left = jnp.where(mine, pltpu.roll(body[plane, 0], head_by, 1), to_left)
            mine = lane8 >> shift == plane
            x_right = tuple(jnp.where(mine, pltpu.roll(xs[sx, plane], tail_by, 1), x_right[sx]) for sx in SIDES)
            x_left = tuple(jnp.where(mine, pltpu.roll(xs[sx, plane], head_by, 1), x_left[sx]) for sx in SIDES)
            return to_right, to_left, x_right, x_left

        none = jnp.zeros((height, LANES), f32)
        to_right, to_left, x_right, x_left = lax.fori_loop(
            0, planes, pack, (none, none, (none8, none8), (none8, none8))
        )
        r["ys"][0], r["ys"][1] = to_right, to_left
        for sx in SIDES:
            r["xys"][0, sx], r["xys"][1, sx] = x_right[sx], x_left[sx]
        groups = height // 8
        for sz in SIDES:
            tail = head = none8
            for k in range(2):
                for group in range(groups):
                    slot = k * groups + group
                    mine = lane8 >> shift == slot
                    part = pl.ds(group * 8, 8)
                    by = (slot * window + window) % LANES
                    tail = jnp.where(mine, pltpu.roll(zs[sz, k, tiles - 1, part, :], by, 1), tail)
                    head = jnp.where(mine, pltpu.roll(zs[sz, k, 0, part, :], slot * window, 1), head)
            r["zys"][0, sz], r["zys"][1, sz] = tail, head
        for sy in SIDES:
            send("y", 16 + sy, r["ys"].at[sy], r["yr"].at[sy], gy=way[sy])
            for s in SIDES:
                send("xy", 18 + 2 * sy + s, r["xys"].at[sy, s], r["xyr"].at[sy, s], gy=way[sy], gx=way[s])
                send("zy", 22 + 2 * sy + s, r["zys"].at[sy, s], r["zyr"].at[sy, s], gy=way[sy], gz=way[s])

    def own_xz(level):
        planes, tiles, height, _ = extent(level)
        body, flat = bodies[level], flat_of(bodies[level])
        groups = height // 8

        def along_x(plane, _):
            for tile in range(tiles):
                lift_rows(flat, (plane * tiles + tile) * height, height)
            return 0

        lax.fori_loop(0, planes, along_x, 0)

        def along_z(block, _):
            tile = block // groups
            part = pl.ds(pl.multiple_of((block % groups) * 8, 8), 8)
            lifted = lift_list([body[plane, tile, part, :] for plane in range(planes)])
            for plane in range(planes):
                body[plane, tile, part, :] = lifted[plane]
            return 0

        lax.fori_loop(0, tiles * groups, along_z, 0)

    def own_y(level):
        planes, tiles, height, _ = extent(level)
        body = bodies[level]
        chunk = min(planes, 512 // height)

        def along_y(number, _):
            where = pl.ds(number * chunk, chunk)
            values = [body[where, tile].reshape(chunk * height, LANES) for tile in range(tiles)]
            lifted = lift_lanes(values, jnp.zeros((chunk * height, LANES), f32), y_weights[level])
            for tile in range(tiles):
                body[where, tile] = lifted[tile].reshape(chunk, height, LANES)
            return 0

        lax.fori_loop(0, planes // chunk, along_y, 0)

    def prepare_y(level):
        height = extent(level)[2]
        r = held[level]
        for sy in SIDES:
            lift_rows(r["yr"].at[sy], 0, height)
            top, low = parts_of(r["yr"][sy])
            stacked = jnp.concatenate([top, low, top], axis=1)
            values = jnp.dot(stacked, z_weights[level][...], preferred_element_type=f32)
            top = values.astype(bf16).astype(f32)
            r["yp"][0, sy] = top
            r["yp"][1, sy] = values - top

    def spread_y(level, planes, pick):
        height = extent(level)[2]
        shift = 2 + level
        yp = held[level]["yp"]
        parts = [[pick(yp.at[part, sy]) for sy in SIDES] for part in range(2)]
        lane = lax.broadcasted_iota(jnp.int32, parts[0][0].shape, 1)
        stacks = []
        for plane in planes:
            mine = lane >> shift == plane
            top, low = [[jnp.where(mine, values, 0.0).astype(bf16) for values in part] for part in parts]
            stacks.append(jnp.concatenate(top + low + top, axis=1))
        return jnp.dot(jnp.concatenate(stacks, axis=0), far_weights[level][...], preferred_element_type=f32)

    def prepare_x(level):
        planes, tiles, height, window = extent(level)
        r = held[level]
        xr, xe, xl = r["xr"], r["xe"], r["xl"]

        def aligned(values):
            return pltpu.roll(values, 9 - tiles, 0) if tiles > 1 else values

        lefts = [aligned(r["xyr"][0, sx]) for sx in SIDES]
        rights = [r["xyr"][1, sx] for sx in SIDES]

        def unpack(plane, _):
            left_by = lax.rem(2 * LANES - window - plane * window, LANES)
            right_by = lax.rem(LANES - plane * window, LANES)
            for sx in SIDES:
                xe[sx, plane] = jnp.where(
                    last_half, pltpu.roll(lefts[sx], left_by, 1), pltpu.roll(rights[sx], right_by, 1)
                )
            return 0

        lax.fori_loop(0, planes, unpack, 0)
        for sx in SIDES:
            halo = [r["er"][sx, sz, k] for sz in SIDES for k in range(2)]
            lifted = lift_list([xr[sx, plane] for plane in range(planes)], halo)
            for plane in range(planes):
                xr[sx, plane] = lifted[plane]
            halo = [
                jnp.where(last_half, aligned(r["cr"][sx, sz, 0, k]), r["cr"][sx, sz, 1, k])
                for sz in SIDES
                for k in range(2)
            ]
            lifted = lift_list([xe[sx, plane] for plane in range(planes)], halo)
            for plane in range(planes):
                xe[sx, plane] = lifted[plane]
        xr_flat, xe_flat = flat_of(xr), flat_of(xe)

        def strip(ref, start):
            return ref[pl.ds(start, 2 * planes, stride=8), :]

        values = [
            jnp.concatenate([strip(xr_flat, k * tiles + tile) for k in range(2)], axis=0) for tile in range(tiles)
        ]
        ext = jnp.concatenate([strip(xe_flat, k * tiles) for k in range(2)], axis=0)
        lifted = lift_lanes(values, ext, y_weights[level])
        for tile in range(tiles):
            xl[tile] = lifted[tile]

    def prepare_z(level):
        planes, tiles, height, window = extent(level)
        r = held[level]
        zr, ze = r["zr"], r["ze"]
        zr_flat, ze_flat = flat_of(zr), flat_of(ze)
        groups = height // 8
        wait_for(level, "zy")
        for sz in SIDES:
            for k in range(2):
                for group in range(groups):
                    slot = k * groups + group
                    left = pltpu.roll(r["zyr"][0, sz], (2 * LANES - window - slot * window) % LANES, 1)
                    right = pltpu.roll(r["zyr"][1, sz], (LANES - slot * window) % LANES, 1)
                    ze[sz, k, pl.ds(group * 8, 8), :] = jnp.where(last_half, left, right)
        wait_for(level, "z")

        def along_x(layer, _):
            for tile in range(tiles):
                lift_rows(zr_flat, (layer * tiles + tile) * height, height)
            lift_rows(ze_flat, layer * height, height)
            return 0

        lax.fori_loop(0, 4, along_x, 0)
        values = [zr[:, :, tile].reshape(4 * height, LANES) for tile in range(tiles)]
        lifted = lift_lanes(values, ze[...].reshape(4 * height, LANES), y_weights[level])
        for tile in range(tiles):
            zr[:, :, tile] = lifted[tile].reshape(2, 2, height, LANES)

    def row_weights(table, layer, at):
        values = none8
        for number, weights in table.items():
            place = at(number)
            if place is not None and weights[layer] != 0.0:
                values = jnp.where(sub == place, weights[layer], values)
        return values

    def add_y(level):
        planes, tiles, height, _ = extent(level)
        body = bodies[level]
        chunk = min(planes, 512 // height)

        def add(number, _):
            where = pl.ds(number * chunk, chunk)
            added = spread_y(level, [number * chunk + inner for inner in range(chunk)], lambda ref: ref[...])
            body[where, 0] = body[where, 0] + added[:, :LANES].reshape(chunk, height, LANES)
            if tiles > 1:
                body[where, tiles - 1] = body[where, tiles - 1] + added[:, LANES:].reshape(chunk, height, LANES)
            return 0

        lax.fori_loop(0, planes // chunk, add, 0)

    def add_x_rows(body, planes, every, height, strips, at):
        tables = ((FROM_LEFT, 0), (FROM_RIGHT, height - 8))
        weigh = [[row_weights(table, layer, at) for layer in range(2)] for table, _ in tables]

        def add(number, _):
            for tile in range(body.shape[1]):
                strip = strips(tile)
                for side in SIDES:
                    part = pl.ds(tables[side][1], 8)
                    first = side * planes + number * every
                    added = weigh[side][0] * strip[pl.ds(first, 1), :]
                    added = added + weigh[side][1] * strip[pl.ds(2 * planes + first, 1), :]
                    body[number, tile, part, :] = body[number, tile, part, :] + added
            return 0

        lax.fori_loop(0, planes // every, add, 0)

    def add_x(level):
        planes, _, height, _ = extent(level)
        xl = held[level]["xl"]
        add_x_rows(bodies[level], planes, 1, height, lambda tile: xl.at[tile], lambda number: number % 8)

    def add_z(level):
        planes, tiles, _, _ = extent(level)
        body, zr = bodies[level], held[level]["zr"]
        for side, table in ((0, FROM_LEFT), (1, FROM_RIGHT)):
            for number, (one, two) in table.items():
                plane = number % planes
                for tile in range(tiles):
                    added = one * zr[side, 0, tile]
                    if two != 0.0:
                        added = added + two * zr[side, 1, tile]
                    body[plane, tile] = body[plane, tile] + added

    start(0)
    for level in range(1, LEVELS):
        make_weights(level)
    own_xz(0)
    planes, tiles, height, _ = extent(0)
    half, deep = height // 2, planes // 2
    inner, inner_tiles = bodies[1], tiles // 2
    flat = flat_of(bodies[0])
    tops = list(range(0, planes, 2))

    def low_rows(ref_flat, start_of):
        return ref_flat[pl.ds(start_of, half, stride=2), :]

    values = [
        jnp.concatenate([low_rows(flat, (plane * tiles + tile) * height) for plane in tops], axis=0)
        for tile in range(tiles)
    ]
    lifted = lift_lanes(values, jnp.zeros((deep * half, LANES), f32), y_weights[0])
    for tile, packed in enumerate(pack_tiles(0, lifted)):
        inner[:, tile] = packed.reshape(deep, half, LANES)

    wait_for(0, "y")
    prepare_y(0)
    added = spread_y(0, tops, lambda ref: ref[pl.ds(0, half, stride=2), :])
    keep = (lax.broadcasted_iota(jnp.int32, (deep * half, LANES), 1) & 1) == 0
    first = jnp.where(keep, added[:, :LANES], 0.0)
    last = jnp.where(keep, 0.0, pltpu.roll(added[:, LANES:], 1, 1))
    inner[:, 0] = inner[:, 0] + first.reshape(deep, half, LANES)
    inner[:, inner_tiles - 1] = inner[:, inner_tiles - 1] + last.reshape(deep, half, LANES)

    wait_for(0, "x", "e", "c", "xy")
    prepare_x(0)
    xl, xp = held[0]["xl"], take()
    for tile, packed in enumerate(pack_tiles(0, [xl[tile] for tile in range(tiles)])):
        xp[tile] = packed

    def even_row(number):
        return (number % 16) // 2 % 8 if number % 2 == 0 else None

    add_x_rows(inner, planes, 2, half, lambda tile: xp.at[tile], even_row)
    prepare_z(0)
    zr_flat = flat_of(held[0]["zr"])
    for side, table in ((0, FROM_LEFT), (1, FROM_RIGHT)):
        packed = [
            pack_tiles(0, [low_rows(zr_flat, ((2 * side + k) * tiles + tile) * height) for tile in range(tiles)])
            for k in range(2)
        ]
        for number, (one, two) in table.items():
            if number % 2 == 0:
                plane = (number % planes) // 2
                for tile in range(inner_tiles):
                    added = one * packed[0][tile]
                    if two != 0.0:
                        added = added + two * packed[1][tile]
                    inner[plane, tile] = inner[plane, tile] + added

    start(1)
    own_xz(1)
    own_y(1)
    own_y(0)
    wait_for(1, "y")
    prepare_y(1)
    add_y(1)
    wait_for(1, "x", "e", "c", "xy")
    prepare_x(1)
    add_x(1)
    prepare_z(1)
    add_z(1)
    planes, tiles, height, _ = extent(1)
    half = height // 2
    flat = flat_of(bodies[1])

    def pick(plane, _):
        values = [flat[pl.ds((2 * plane * tiles + tile) * height, half, stride=2), :] for tile in range(tiles)]
        for tile, packed in enumerate(pack_tiles(1, values)):
            bodies[2][plane, tile] = packed
        return 0

    lax.fori_loop(0, planes // 2, pick, 0)

    start(2)
    own_xz(2)
    own_y(2)
    add_y(0)
    add_x(0)
    add_z(0)
    wait_for(2, "y")
    prepare_y(2)
    add_y(2)
    wait_for(2, "x", "e", "c", "xy")
    prepare_x(2)
    add_x(2)
    prepare_z(2)
    add_z(2)

    for level in (1, 0):
        planes, tiles, height, _ = extent(level)
        half = height // 2
        flat = flat_of(bodies[level])

        def place(plane, _):
            where = [pl.ds((2 * plane * tiles + tile) * height, half, stride=2) for tile in range(tiles)]
            inner = [bodies[level + 1][plane, tile] for tile in range(tiles // 2)]
            for at, values in zip(where, unpack_tiles(level, [flat[at, :] for at in where], inner)):
                flat[at, :] = values
            return 0

        lax.fori_loop(0, planes // 2, place, 0)

    for copy in sends:
        copy.wait_send()


def write_out(held_ref, out_ref, sem):
    copies = [
        pltpu.make_async_copy(held_ref.at[:, tile], out_ref.at[:, :, pl.ds(tile * LANES, LANES)], sem.at[tile])
        for tile in range(TILES)
    ]
    for copy in copies:
        copy.start()
    for copy in copies:
        copy.wait()


def local(field):
    depth, rows, lanes = field.shape
    vmem = pltpu.VMEM
    sizes = [(depth >> level, TILES >> level, rows >> level) for level in range(LEVELS)]
    scratch = [vmem((planes, tiles, height, LANES), f32) for planes, tiles, height in sizes[1:]]
    scratch += [
        pltpu.SemaphoreType.DMA((TILES,)),
        pltpu.SemaphoreType.DMA((LEVELS, 26)),
        pltpu.SemaphoreType.DMA((LEVELS, 26)),
    ]
    widths = [min(tiles, 2) * LANES for _, tiles, _ in sizes]
    scratch += [vmem((3 * (width + LANES), width), bf16) for width in widths]
    scratch += [vmem((6 * LANES, width), bf16) for width in widths]
    scratch += [vmem((3 * LANES, LANES), bf16) for _ in sizes]
    for planes, tiles, height in sizes:
        shapes = [(2, 2, tiles, height)] * 2 + [(2, 2, height)]
        shapes += [(2, planes, 8)] * 3 + [(tiles, 4 * planes)]
        shapes += [(2, 2, 2, 8)] * 2 + [(2, height)] * 2 + [(2, 2, height)]
        shapes += [(2, 2, 8)] * 4 + [(2, 2, 2, 2, 8)]
        scratch += [vmem((*shape, LANES), f32) for shape in shapes]
    scratch += [vmem((TILES // 2, 4 * depth, LANES), f32)]
    lifted = pl.pallas_call(
        functools.partial(kernel, field.shape),
        out_shape=jax.ShapeDtypeStruct((depth, TILES, rows, LANES), f32),
        in_specs=[pl.BlockSpec(memory_space=pltpu.HBM)],
        out_specs=pl.BlockSpec(memory_space=pltpu.VMEM),
        scratch_shapes=scratch,
        compiler_params=pltpu.CompilerParams(
            collective_id=0, has_side_effects=True, vmem_limit_bytes=48 * 2**20
        ),
        name="lift",
    )(field)
    return pl.pallas_call(
        write_out,
        out_shape=jax.ShapeDtypeStruct(field.shape, f32),
        in_specs=[pl.BlockSpec(memory_space=pltpu.VMEM)],
        out_specs=pl.BlockSpec(memory_space=pltpu.HBM),
        scratch_shapes=[pltpu.SemaphoreType.DMA((TILES,))],
        compiler_params=pltpu.CompilerParams(vmem_limit_bytes=8 * 2**20),
        name="write_out",
    )(lifted)


def solution(mesh):
    placed = (P("gz", "gx", "gy"),)
    return jax.shard_map(
        local, mesh=mesh, in_specs=placed, out_specs=P("gz", "gx", "gy"), check_vma=False
    )
```

time: 49.9 us -> 45.6 us (0.914)
  local copies, waits for them, and re-layouts: 2.19 us -> 0 us
  Pallas kernels: 47.6 us -> 45.5 us
    unnamed x2 -> x0, local copies, waits for them, and re-layouts: 2.19 us -> none
    pallas_call x1, Pallas kernels: 45.5 us -> 43.5 us  [local(): pl.pallas_call(functools.partial(kernel, field.shape), out_shape=jax.Shap...]
where the time goes in v1:
time: 45.6 us; the launch traced here: 45.5 us
  Pallas kernels  45.5 us (100%)
    pallas_call x1, Pallas kernels, local(): pl.pallas_call(functools.partial(kernel, field.shape), out_shape=jax.Shap...  43.5 us
    pallas_call x1, Pallas kernels, local(): pl.pallas_call(write_out, out_shape=jax.ShapeDtypeStruct(field.shape, f32...  2.04 us

profile of v1, /device:TPU:1, one launch (start us, length us, event | category | flops | bytes accessed | tf_op | source)
XLA Modules:
  0.0 45.5 jit_solution(10778852931891453394)
XLA Ops:
  0.0 43.5 %lift.1.held_ref = f32[32,4,64,128]{3,2,1,0:T(8,128)S(1)} custom-call(f32[32,64,512]{2,1,0:T(8,128)} %field_ref.1), custom_call_target="tpu_custom_call" | custom-call | tf_op jit(solution)/shard_map/lift/pallas_call | solution.py:705
  43.5 2.0 %write_out.1 = f32[32,64,512]{2,1,0:T(8,128)} custom-call(f32[32,4,64,128]{3,2,1,0:T(8,128)S(1)} %lift.1.held_ref), custom_call_target="tpu_custom_call" | custom-call | tf_op jit(solution)/shard_map/write_out/pallas_call | solution.py:716

commit v2 on v1

--- a/solution.py
+++ b/solution.py
@@ -165,14 +165,25 @@
     return out
 
 
+def loop(count, unroll, body, carry=0):
+    unroll = min(unroll, count)
+
+    def turns(number, carried):
+        for inner in range(unroll):
+            carried = body(number * unroll + inner, carried)
+        return carried
+
+    return lax.fori_loop(0, count // unroll, turns, carry)
+
+
 NAMES = ("zs", "zr", "ze", "xs", "xr", "xe", "xl", "es", "er", "ys", "yr", "yp", "zys", "zyr", "xys", "xyr", "cr")
 
 
-def kernel(shape, field_ref, out_ref, *scratch):
+def kernel(shape, field_ref, out_ref, inner_ref, *scratch):
     depth, rows, _ = shape
     refs = list(scratch)
     take = lambda: refs.pop(0)
-    bodies = [out_ref, take(), take()]
+    bodies = [out_ref, inner_ref, take()]
     load_sem, send_sem, recv_sem = take(), take(), take()
     y_weights, far_weights, z_weights = [[take() for _ in range(LEVELS)] for _ in range(3)]
     held = [{name: take() for name in NAMES} for _ in range(LEVELS)]
@@ -180,8 +191,13 @@
     here = {name: lax.axis_index(name) for name in ("gx", "gy", "gz")}
     count = {name: lax.axis_size(name) for name in ("gx", "gy", "gz")}
 
+    near = {
+        name: {-1: lax.rem(at + count[name] - 1, count[name]), 0: at, 1: lax.rem(at + 1, count[name])}
+        for name, at in here.items()
+    }
+
     def beside(**by):
-        return {name: lax.rem(here[name] + way + count[name], count[name]) for name, way in by.items()}
+        return {name: near[name][way] for name, way in by.items()}
 
     barrier = pltpu.get_barrier_semaphore()
     for x in (-1, 0, 1):
@@ -339,8 +355,8 @@
             return to_right, to_left, x_right, x_left
 
         none = jnp.zeros((height, LANES), f32)
-        to_right, to_left, x_right, x_left = lax.fori_loop(
-            0, planes, pack, (none, none, (none8, none8), (none8, none8))
+        to_right, to_left, x_right, x_left = loop(
+            planes, 4, pack, (none, none, (none8, none8), (none8, none8))
         )
         r["ys"][0], r["ys"][1] = to_right, to_left
         for sx in SIDES:
@@ -373,7 +389,7 @@
                 lift_rows(flat, (plane * tiles + tile) * height, height)
             return 0
 
-        lax.fori_loop(0, planes, along_x, 0)
+        loop(planes, 2 if level == 0 else 4, along_x)
 
         def along_z(block, _):
             tile = block // groups
@@ -383,7 +399,7 @@
                 body[plane, tile, part, :] = lifted[plane]
             return 0
 
-        lax.fori_loop(0, tiles * groups, along_z, 0)
+        loop(tiles * groups, 1 if level == 0 else 2, along_z)
 
     def own_y(level):
         planes, tiles, height, _ = extent(level)
@@ -445,7 +461,7 @@
                 )
             return 0
 
-        lax.fori_loop(0, planes, unpack, 0)
+        loop(planes, 8, unpack)
         for sx in SIDES:
             halo = [r["er"][sx, sz, k] for sz in SIDES for k in range(2)]
             lifted = lift_list([xr[sx, plane] for plane in range(planes)], halo)
@@ -494,7 +510,7 @@
             lift_rows(ze_flat, layer * height, height)
             return 0
 
-        lax.fori_loop(0, 4, along_x, 0)
+        loop(4, 4, along_x)
         values = [zr[:, :, tile].reshape(4 * height, LANES) for tile in range(tiles)]
         lifted = lift_lanes(values, ze[...].reshape(4 * height, LANES), y_weights[level])
         for tile in range(tiles):
@@ -538,7 +554,7 @@
                     body[number, tile, part, :] = body[number, tile, part, :] + added
             return 0
 
-        lax.fori_loop(0, planes // every, add, 0)
+        loop(planes // every, 4, add)
 
     def add_x(level):
         planes, _, height, _ = extent(level)
@@ -635,7 +651,7 @@
             bodies[2][plane, tile] = packed
         return 0
 
-    lax.fori_loop(0, planes // 2, pick, 0)
+    loop(planes // 2, 4, pick)
 
     start(2)
     own_xz(2)
@@ -652,40 +668,67 @@
     prepare_z(2)
     add_z(2)
 
-    for level in (1, 0):
-        planes, tiles, height, _ = extent(level)
-        half = height // 2
-        flat = flat_of(bodies[level])
-
-        def place(plane, _):
-            where = [pl.ds((2 * plane * tiles + tile) * height, half, stride=2) for tile in range(tiles)]
-            inner = [bodies[level + 1][plane, tile] for tile in range(tiles // 2)]
-            for at, values in zip(where, unpack_tiles(level, [flat[at, :] for at in where], inner)):
-                flat[at, :] = values
-            return 0
-
-        lax.fori_loop(0, planes // 2, place, 0)
+    planes, tiles, height, _ = extent(1)
+    half = height // 2
+
+    def place(plane, _):
+        where = [pl.ds((2 * plane * tiles + tile) * height, half, stride=2) for tile in range(tiles)]
+        inner = [bodies[2][plane, tile] for tile in range(tiles // 2)]
+        for at, values in zip(where, unpack_tiles(1, [flat[at, :] for at in where], inner)):
+            flat[at, :] = values
+        return 0
+
+    loop(planes // 2, 4, place)
 
     for copy in sends:
         copy.wait_send()
 
 
-def write_out(held_ref, out_ref, sem):
-    copies = [
-        pltpu.make_async_copy(held_ref.at[:, tile], out_ref.at[:, :, pl.ds(tile * LANES, LANES)], sem.at[tile])
-        for tile in range(TILES)
-    ]
-    for copy in copies:
-        copy.start()
-    for copy in copies:
-        copy.wait()
+def write_out(held_ref, inner_ref, out_ref, merged, sem):
+    depth, tiles, rows, _ = held_ref.shape
+    planes, half = depth // 2, rows // 2
+    pairs = held_ref.reshape(planes, 2, tiles, rows, LANES)
+    target = out_ref.reshape(planes, 2, rows, tiles * LANES)
+    parts = sem.shape[0] - 1
+    size = planes // parts
+
+    def copy(source, odd, tile, slot, where):
+        return pltpu.make_async_copy(
+            source, target.at[where, odd, :, pl.ds(tile * LANES, LANES)], sem.at[slot, tile]
+        )
+
+    copies = [copy(pairs.at[:, 1, tile], 1, tile, parts, pl.ds(0, planes)) for tile in range(tiles)]
+    for one in copies:
+        one.start()
+    held_flat = held_ref.reshape(depth * tiles * rows, LANES)
+    merged_flat = merged.reshape(planes * tiles * rows, LANES)
+
+    def place(plane, _):
+        source = [2 * plane * tiles * rows + tile * rows for tile in range(tiles)]
+        target = [plane * tiles * rows + tile * rows for tile in range(tiles)]
+        low = [held_flat[pl.ds(start, half, stride=2), :] for start in source]
+        inner = [inner_ref[plane, tile] for tile in range(tiles // 2)]
+        for tile, values in enumerate(unpack_tiles(0, low, inner)):
+            merged_flat[pl.ds(target[tile], half, stride=2), :] = values
+            odd = held_flat[pl.ds(source[tile] + 1, half, stride=2), :]
+            merged_flat[pl.ds(target[tile] + 1, half, stride=2), :] = odd
+        return 0
+
+    for part in range(parts):
+        loop(size, 4, lambda number, _: place(part * size + number, _))
+        for tile in range(tiles):
+            where = pl.ds(part * size, size)
+            copies.append(copy(merged.at[where, tile], 0, tile, part, where))
+            copies[-1].start()
+    for one in copies:
+        one.wait()
 
 
 def local(field):
     depth, rows, lanes = field.shape
     vmem = pltpu.VMEM
     sizes = [(depth >> level, TILES >> level, rows >> level) for level in range(LEVELS)]
-    scratch = [vmem((planes, tiles, height, LANES), f32) for planes, tiles, height in sizes[1:]]
+    scratch = [vmem((planes, tiles, height, LANES), f32) for planes, tiles, height in sizes[2:]]
     scratch += [
         pltpu.SemaphoreType.DMA((TILES,)),
         pltpu.SemaphoreType.DMA((LEVELS, 26)),
@@ -704,9 +747,9 @@
     scratch += [vmem((TILES // 2, 4 * depth, LANES), f32)]
     lifted = pl.pallas_call(
         functools.partial(kernel, field.shape),
-        out_shape=jax.ShapeDtypeStruct((depth, TILES, rows, LANES), f32),
+        out_shape=[jax.ShapeDtypeStruct((size[0], size[1], size[2], LANES), f32) for size in sizes[:2]],
         in_specs=[pl.BlockSpec(memory_space=pltpu.HBM)],
-        out_specs=pl.BlockSpec(memory_space=pltpu.VMEM),
+        out_specs=[pl.BlockSpec(memory_space=pltpu.VMEM)] * 2,
         scratch_shapes=scratch,
         compiler_params=pltpu.CompilerParams(
             collective_id=0, has_side_effects=True, vmem_limit_bytes=48 * 2**20
@@ -716,12 +759,15 @@
     return pl.pallas_call(
         write_out,
         out_shape=jax.ShapeDtypeStruct(field.shape, f32),
-        in_specs=[pl.BlockSpec(memory_space=pltpu.VMEM)],
+        in_specs=[pl.BlockSpec(memory_space=pltpu.VMEM)] * 2,
         out_specs=pl.BlockSpec(memory_space=pltpu.HBM),
-        scratch_shapes=[pltpu.SemaphoreType.DMA((TILES,))],
+        scratch_shapes=[
+            vmem((depth // 2, TILES, rows, LANES), f32),
+            pltpu.SemaphoreType.DMA((3, TILES)),
+        ],
         compiler_params=pltpu.CompilerParams(vmem_limit_bytes=8 * 2**20),
         name="write_out",
-    )(lifted)
+    )(*lifted)
 
 
 def solution(mesh):

time: 45.6 us -> 37.2 us (0.82)
  Pallas kernels: 45.5 us -> 37.1 us
    pallas_call x1, Pallas kernels: 43.5 us -> 35 us  [local(): pl.pallas_call(functools.partial(kernel, field.shape), out_shape=[jax.Sha...]
where the time goes in v2:
time: 37.2 us; the launch traced here: 37.1 us
  Pallas kernels  37.1 us (100%)
    pallas_call x1, Pallas kernels, local(): pl.pallas_call(functools.partial(kernel, field.shape), out_shape=[jax.Sha...  35 us
    pallas_call x1, Pallas kernels, local(): pl.pallas_call(write_out, out_shape=jax.ShapeDtypeStruct(field.shape, f32...  2.11 us

profile of v2, /device:TPU:1, one launch (start us, length us, event | category | flops | bytes accessed | tf_op | source)
XLA Modules:
  0.0 37.1 jit_solution(10656770735658848041)
XLA Ops:
  0.0 35.0 %lift.1 = (f32[32,4,64,128]{3,2,1,0:T(8,128)S(1)}, f32[16,2,32,128]{3,2,1,0:T(8,128)S(1)}) custom-call(f32[32,64,512]{2,1,0:T(8,128)} %field_ref.1), custom_call_target="tpu_custom_call" | custom-call | tf_op jit(solution)/shard_map/lift/pallas_call | solution.py:748
  35.0 2.1 %write_out.1 = f32[32,64,512]{2,1,0:T(8,128)} custom-call(f32[32,4,64,128]{3,2,1,0:T(8,128)S(1)} %get-tuple-element.7.held_ref, f32[16,2,32,128]{3,2,1,0:T(8,128)S(1)} %get-tuple-element.8.inner_ref), custom_call_target="tpu_custom_call" | custom-call | tf_op jit(solution)/shard_map/write_out/pallas_call | solution.py:759

commit v3 on v2

--- a/solution.py
+++ b/solution.py
@@ -177,6 +177,7 @@
 
 
 NAMES = ("zs", "zr", "ze", "xs", "xr", "xe", "xl", "es", "er", "ys", "yr", "yp", "zys", "zyr", "xys", "xyr", "cr")
+FIRST_NAMES = ("zl", "zc", "zlow", "zlowr")
 
 
 def kernel(shape, field_ref, out_ref, inner_ref, *scratch):
@@ -187,6 +188,7 @@
     load_sem, send_sem, recv_sem = take(), take(), take()
     y_weights, far_weights, z_weights = [[take() for _ in range(LEVELS)] for _ in range(3)]
     held = [{name: take() for name in NAMES} for _ in range(LEVELS)]
+    held[0].update({name: take() for name in FIRST_NAMES})
 
     here = {name: lax.axis_index(name) for name in ("gx", "gy", "gz")}
     count = {name: lax.axis_size(name) for name in ("gx", "gy", "gz")}
@@ -207,13 +209,19 @@
                     pl.semaphore_signal(barrier, inc=1, device_id=beside(gx=x, gy=y, gz=z), device_id_type=MESH)
 
     loads = [
-        pltpu.make_async_copy(
-            field_ref.at[:, :, pl.ds(tile * LANES, LANES)], out_ref.at[:, tile], load_sem.at[tile]
-        )
-        for tile in range(TILES)
+        [
+            pltpu.make_async_copy(
+                field_ref.at[pl.ds(first, size), :, pl.ds(tile * LANES, LANES)],
+                out_ref.at[pl.ds(first, size), tile],
+                load_sem.at[number, tile],
+            )
+            for tile in range(TILES)
+        ]
+        for number, (first, size) in enumerate(((0, 4), (depth - 4, 4), (4, depth - 8)))
     ]
-    for load in loads:
-        load.start()
+    for part in loads:
+        for load in part:
+            load.start()
 
     def fill(ref, blocks):
         start = 0
@@ -258,8 +266,9 @@
         fill(z_weights[level], [jnp.where((row & (window - 1)) == (col & (window - 1)), taps, 0.0)])
 
     make_weights(0)
-    for load in loads:
-        load.wait()
+    for part in loads[:2]:
+        for load in part:
+            load.wait()
 
     sends = []
     arrivals = [{} for _ in range(LEVELS)]
@@ -282,6 +291,30 @@
         for key in keys:
             for copy in arrivals[level][key]:
                 copy.wait_recv()
+
+    def lift_layers(layers, low):
+        _, tiles, height, _ = extent(0)
+        layers_flat = flat_of(layers)
+
+        def along_x(layer, _):
+            for tile in range(tiles):
+                lift_rows(layers_flat, (layer * tiles + tile) * height, height)
+            return 0
+
+        loop(4, 4, along_x)
+        values = [layers[:, :, tile].reshape(4 * height, LANES) for tile in range(tiles)]
+        lifted = lift_lanes(values, jnp.zeros((4 * height, LANES), f32), y_weights[0])
+        for tile in range(tiles):
+            layers[:, :, tile] = lifted[tile].reshape(2, 2, height, LANES)
+        for layer in range(4):
+            for tile, packed in enumerate(pack_tiles(0, low_tiles(layers_flat, layer))):
+                low[layer // 2, layer % 2, tile] = packed
+
+    def low_tiles(layers_flat, layer):
+        _, tiles, height, _ = extent(0)
+        return [
+            layers_flat[pl.ds((layer * tiles + tile) * height, height // 2, stride=2), :] for tile in range(tiles)
+        ]
 
     def start(level):
         planes, tiles, height, window = extent(level)
@@ -297,7 +330,7 @@
                 device_id=beside(**by),
                 device_id_type=MESH,
             )
-            if level == 0 and number == 0:
+            if not sends:
                 pl.semaphore_wait(barrier, 26)
             copy.start()
             sends.append(copy)
@@ -310,8 +343,18 @@
             for k in range(2):
                 zs[0, k, tile] = end[k]
                 zs[1, k, tile] = begin[k]
-        for side in SIDES:
-            send("z", side, zs.at[side], r["zr"].at[side], gz=way[side])
+                if level == 0:
+                    r["zl"][0, k, tile] = end[k]
+                    r["zl"][1, k, tile] = begin[k]
+        if level == 0:
+            lift_layers(r["zl"], r["zlow"])
+            for side in SIDES:
+                send("zlow", 26 + side, r["zlow"].at[side], r["zlowr"].at[side], gz=way[side])
+            for load in loads[2]:
+                load.wait()
+        else:
+            for side in SIDES:
+                send("z", side, zs.at[side], r["zr"].at[side], gz=way[side])
 
         xs_flat = flat_of(xs)
         for tile in range(tiles):
@@ -378,11 +421,13 @@
             for s in SIDES:
                 send("xy", 18 + 2 * sy + s, r["xys"].at[sy, s], r["xyr"].at[sy, s], gy=way[sy], gx=way[s])
                 send("zy", 22 + 2 * sy + s, r["zys"].at[sy, s], r["zyr"].at[sy, s], gy=way[sy], gz=way[s])
-
-    def own_xz(level):
+        if level == 0:
+            for side in SIDES:
+                send("z", side, r["zl"].at[side], r["zr"].at[side], gz=way[side])
+
+    def own_x(level):
         planes, tiles, height, _ = extent(level)
-        body, flat = bodies[level], flat_of(bodies[level])
-        groups = height // 8
+        flat = flat_of(bodies[level])
 
         def along_x(plane, _):
             for tile in range(tiles):
@@ -391,17 +436,28 @@
 
         loop(planes, 2 if level == 0 else 4, along_x)
 
+    def own_z(level, parity=None):
+        planes, tiles, height, _ = extent(level)
+        flat = flat_of(bodies[level])
+        every = 1 if parity is None else 2
+        groups = height // (8 * every)
+
         def along_z(block, _):
-            tile = block // groups
-            part = pl.ds(pl.multiple_of((block % groups) * 8, 8), 8)
-            lifted = lift_list([body[plane, tile, part, :] for plane in range(planes)])
-            for plane in range(planes):
-                body[plane, tile, part, :] = lifted[plane]
+            tile, group = block // groups, block % groups
+            first = tile * height + group * 8 * every
+            if parity is None:
+                first = pl.multiple_of(first, 8)
+                where = [pl.ds(first + plane * tiles * height, 8) for plane in range(planes)]
+            else:
+                where = [pl.ds(first + parity + plane * tiles * height, 8, stride=2) for plane in range(planes)]
+            lifted = lift_list([flat[at, :] for at in where])
+            for at, values in zip(where, lifted):
+                flat[at, :] = values
             return 0
 
         loop(tiles * groups, 1 if level == 0 else 2, along_z)
 
-    def own_y(level):
+    def own_y(level, start=0, stop=None):
         planes, tiles, height, _ = extent(level)
         body = bodies[level]
         chunk = min(planes, 512 // height)
@@ -414,7 +470,7 @@
                 body[where, tile] = lifted[tile].reshape(chunk, height, LANES)
             return 0
 
-        lax.fori_loop(0, planes // chunk, along_y, 0)
+        lax.fori_loop(start, planes // chunk if stop is None else stop, along_y, 0)
 
     def prepare_y(level):
         height = extent(level)[2]
@@ -502,6 +558,20 @@
                     left = pltpu.roll(r["zyr"][0, sz], (2 * LANES - window - slot * window) % LANES, 1)
                     right = pltpu.roll(r["zyr"][1, sz], (LANES - slot * window) % LANES, 1)
                     ze[sz, k, pl.ds(group * 8, 8), :] = jnp.where(last_half, left, right)
+        if level == 0:
+            for layer in range(4):
+                lift_rows(ze_flat, layer * height, height)
+            ext = ze[...].reshape(4 * height, LANES)
+            first = lax.broadcasted_iota(jnp.int32, ext.shape, 1) < LANES // 2
+            side_weights = y_weights[0][6 * LANES :]
+            for block in range(2):
+                top, low = parts_of(jnp.where(first, 0.0, ext) if block == 0 else jnp.where(first, ext, 0.0))
+                stacked = jnp.concatenate([top, low, top], axis=1)
+                added = jnp.dot(stacked, side_weights, preferred_element_type=f32)
+                for tile in range(2):
+                    part = added[:, tile * LANES : (tile + 1) * LANES]
+                    r["zc"][:, :, 2 * block + tile] = part.reshape(2, 2, height, LANES)
+            return
         wait_for(level, "z")
 
         def along_x(layer, _):
@@ -564,6 +634,12 @@
     def add_z(level):
         planes, tiles, _, _ = extent(level)
         body, zr = bodies[level], held[level]["zr"]
+        if level == 0:
+            wait_for(0, "z")
+            for side in SIDES:
+                for k in range(2):
+                    for tile in range(tiles):
+                        zr[side, k, tile] = zr[side, k, tile] + held[0]["zc"][side, k, tile]
         for side, table in ((0, FROM_LEFT), (1, FROM_RIGHT)):
             for number, (one, two) in table.items():
                 plane = number % planes
@@ -574,9 +650,8 @@
                     body[plane, tile] = body[plane, tile] + added
 
     start(0)
-    for level in range(1, LEVELS):
-        make_weights(level)
-    own_xz(0)
+    own_x(0)
+    own_z(0, 0)
     planes, tiles, height, _ = extent(0)
     half, deep = height // 2, planes // 2
     inner, inner_tiles = bodies[1], tiles // 2
@@ -614,10 +689,12 @@
 
     add_x_rows(inner, planes, 2, half, lambda tile: xp.at[tile], even_row)
     prepare_z(0)
-    zr_flat = flat_of(held[0]["zr"])
+    zc_flat = flat_of(held[0]["zc"])
+    packed_layers = [pack_tiles(0, low_tiles(zc_flat, layer)) for layer in range(4)]
+    wait_for(0, "zlow")
     for side, table in ((0, FROM_LEFT), (1, FROM_RIGHT)):
         packed = [
-            pack_tiles(0, [low_rows(zr_flat, ((2 * side + k) * tiles + tile) * height) for tile in range(tiles)])
+            [held[0]["zlowr"][side, k, tile] + packed_layers[2 * side + k][tile] for tile in range(inner_tiles)]
             for k in range(2)
         ]
         for number, (one, two) in table.items():
@@ -630,9 +707,12 @@
                     inner[plane, tile] = inner[plane, tile] + added
 
     start(1)
-    own_xz(1)
+    make_weights(1)
+    own_x(1)
+    own_z(1)
     own_y(1)
-    own_y(0)
+    own_z(0, 1)
+    own_y(0, 0, 2)
     wait_for(1, "y")
     prepare_y(1)
     add_y(1)
@@ -654,8 +734,11 @@
     loop(planes // 2, 4, pick)
 
     start(2)
-    own_xz(2)
+    make_weights(2)
+    own_x(2)
+    own_z(2)
     own_y(2)
+    own_y(0, 2)
     add_y(0)
     add_x(0)
     add_z(0)
@@ -730,9 +813,9 @@
     sizes = [(depth >> level, TILES >> level, rows >> level) for level in range(LEVELS)]
     scratch = [vmem((planes, tiles, height, LANES), f32) for planes, tiles, height in sizes[2:]]
     scratch += [
-        pltpu.SemaphoreType.DMA((TILES,)),
-        pltpu.SemaphoreType.DMA((LEVELS, 26)),
-        pltpu.SemaphoreType.DMA((LEVELS, 26)),
+        pltpu.SemaphoreType.DMA((3, TILES)),
+        pltpu.SemaphoreType.DMA((LEVELS, 28)),
+        pltpu.SemaphoreType.DMA((LEVELS, 28)),
     ]
     widths = [min(tiles, 2) * LANES for _, tiles, _ in sizes]
     scratch += [vmem((3 * (width + LANES), width), bf16) for width in widths]
@@ -744,6 +827,7 @@
         shapes += [(2, 2, 2, 8)] * 2 + [(2, height)] * 2 + [(2, 2, height)]
         shapes += [(2, 2, 8)] * 4 + [(2, 2, 2, 2, 8)]
         scratch += [vmem((*shape, LANES), f32) for shape in shapes]
+    scratch += [vmem((2, 2, TILES, rows, LANES), f32)] * 2 + [vmem((2, 2, TILES // 2, rows // 2, LANES), f32)] * 2
     scratch += [vmem((TILES // 2, 4 * depth, LANES), f32)]
     lifted = pl.pallas_call(
         functools.partial(kernel, field.shape),

time: 37.2 us -> 35.7 us (0.960)
  Pallas kernels: 37.1 us -> 35.7 us
    pallas_call x1, Pallas kernels: 35 us -> 33.6 us  [local(): pl.pallas_call(functools.partial(kernel, field.shape), out_shape=[jax.Sha...]
where the time goes in v3:
time: 35.7 us
  Pallas kernels  35.7 us (100%)
    pallas_call x1, Pallas kernels, local(): pl.pallas_call(functools.partial(kernel, field.shape), out_shape=[jax.Sha...  33.6 us
    pallas_call x1, Pallas kernels, local(): pl.pallas_call(write_out, out_shape=jax.ShapeDtypeStruct(field.shape, f32...  2.11 us

profile of v3, /device:TPU:1, one launch (start us, length us, event | category | flops | bytes accessed | tf_op | source)
XLA Modules:
  0.0 35.7 jit_solution(5520643950090827189)
XLA Ops:
  0.0 33.6 %lift.1 = (f32[32,4,64,128]{3,2,1,0:T(8,128)S(1)}, f32[16,2,32,128]{3,2,1,0:T(8,128)S(1)}) custom-call(f32[32,64,512]{2,1,0:T(8,128)} %field_ref.1), custom_call_target="tpu_custom_call" | custom-call | tf_op jit(solution)/shard_map/lift/pallas_call | solution.py:832
  33.6 2.1 %write_out.1 = f32[32,64,512]{2,1,0:T(8,128)} custom-call(f32[32,4,64,128]{3,2,1,0:T(8,128)S(1)} %get-tuple-element.7.held_ref, f32[16,2,32,128]{3,2,1,0:T(8,128)S(1)} %get-tuple-element.8.inner_ref), custom_call_target="tpu_custom_call" | custom-call | tf_op jit(solution)/shard_map/write_out/pallas_call | solution.py:843

commit v4 on v3

--- a/solution.py
+++ b/solution.py
@@ -177,6 +177,7 @@
 
 
 NAMES = ("zs", "zr", "ze", "xs", "xr", "xe", "xl", "es", "er", "ys", "yr", "yp", "zys", "zyr", "xys", "xyr", "cr")
+GROUPS = {"y": 0, "x": 1, "e": 1, "c": 1, "xy": 1, "zy": 2, "z": 3, "zlow": 4}
 FIRST_NAMES = ("zl", "zc", "zlow", "zlowr")
 
 
@@ -270,8 +271,8 @@
         for load in part:
             load.wait()
 
-    sends = []
-    arrivals = [{} for _ in range(LEVELS)]
+    sent = [0] * LEVELS
+    arriving = [[0] * 5 for _ in range(LEVELS)]
     way = (1, -1)
     sub = lax.broadcasted_iota(jnp.int32, (8, LANES), 0)
     lane8 = lax.broadcasted_iota(jnp.int32, (8, LANES), 1)
@@ -287,10 +288,12 @@
             size *= extent_of_dim
         return ref.reshape(size, LANES)
 
-    def wait_for(level, *keys):
-        for key in keys:
-            for copy in arrivals[level][key]:
-                copy.wait_recv()
+    def wait_rows(sem, count):
+        held_rows = flat_of(out_ref).at[pl.ds(0, count)]
+        pltpu.make_async_copy(held_rows, held_rows, sem).wait()
+
+    def wait_for(level, key):
+        wait_rows(recv_sem.at[level, GROUPS[key]], arriving[level][GROUPS[key]])
 
     def lift_layers(layers, low):
         _, tiles, height, _ = extent(0)
@@ -321,20 +324,23 @@
         body, flat, r = bodies[level], flat_of(bodies[level]), held[level]
         shift = 2 + level
 
-        def send(key, number, source, target, **by):
+        def send(key, source, target, **by):
             copy = pltpu.make_async_remote_copy(
                 src_ref=source,
                 dst_ref=target,
-                send_sem=send_sem.at[level, number],
-                recv_sem=recv_sem.at[level, number],
+                send_sem=send_sem.at[level],
+                recv_sem=recv_sem.at[level, GROUPS[key]],
                 device_id=beside(**by),
                 device_id_type=MESH,
             )
-            if not sends:
+            if level == 0 and not sent[0]:
                 pl.semaphore_wait(barrier, 26)
             copy.start()
-            sends.append(copy)
-            arrivals[level].setdefault(key, []).append(copy)
+            size = 1
+            for extent_of_dim in source.shape[:-1]:
+                size *= extent_of_dim
+            sent[level] += size
+            arriving[level][GROUPS[key]] += size
 
         zs, xs, es = r["zs"], r["xs"], r["es"]
         for tile in range(tiles):
@@ -349,12 +355,12 @@
         if level == 0:
             lift_layers(r["zl"], r["zlow"])
             for side in SIDES:
-                send("zlow", 26 + side, r["zlow"].at[side], r["zlowr"].at[side], gz=way[side])
+                send("zlow", r["zlow"].at[side], r["zlowr"].at[side], gz=way[side])
             for load in loads[2]:
                 load.wait()
         else:
             for side in SIDES:
-                send("z", side, zs.at[side], r["zr"].at[side], gz=way[side])
+                send("z", zs.at[side], r["zr"].at[side], gz=way[side])
 
         xs_flat = flat_of(xs)
         for tile in range(tiles):
@@ -367,7 +373,7 @@
                 xs_flat[pl.ds(k * tiles + tile, planes, stride=8), :] = end[k]
                 xs_flat[pl.ds(planes * 8 + k * tiles + tile, planes, stride=8), :] = begin[k]
         for side in SIDES:
-            send("x", 2 + side, xs.at[side], r["xr"].at[side], gx=way[side])
+            send("x", xs.at[side], r["xr"].at[side], gx=way[side])
 
         for side in SIDES:
             end = encode_end(*[xs[side, planes - 4 + number] for number in range(4)])
@@ -377,11 +383,9 @@
                 es[side, 1, k] = begin[k]
         for sx in SIDES:
             for sz in SIDES:
-                number = 4 + 2 * sx + sz
-                send("e", number, es.at[sx, sz], r["er"].at[sx, sz], gx=way[sx], gz=way[sz])
+                send("e", es.at[sx, sz], r["er"].at[sx, sz], gx=way[sx], gz=way[sz])
                 for sy in SIDES:
-                    number = 8 + 4 * sx + 2 * sz + sy
-                    send("c", number, es.at[sx, sz], r["cr"].at[sx, sz, sy], gx=way[sx], gz=way[sz], gy=way[sy])
+                    send("c", es.at[sx, sz], r["cr"].at[sx, sz, sy], gx=way[sx], gz=way[sz], gy=way[sy])
 
         lane = lax.broadcasted_iota(jnp.int32, (height, LANES), 1)
 
@@ -417,13 +421,13 @@
                     head = jnp.where(mine, pltpu.roll(zs[sz, k, 0, part, :], slot * window, 1), head)
             r["zys"][0, sz], r["zys"][1, sz] = tail, head
         for sy in SIDES:
-            send("y", 16 + sy, r["ys"].at[sy], r["yr"].at[sy], gy=way[sy])
+            send("y", r["ys"].at[sy], r["yr"].at[sy], gy=way[sy])
             for s in SIDES:
-                send("xy", 18 + 2 * sy + s, r["xys"].at[sy, s], r["xyr"].at[sy, s], gy=way[sy], gx=way[s])
-                send("zy", 22 + 2 * sy + s, r["zys"].at[sy, s], r["zyr"].at[sy, s], gy=way[sy], gz=way[s])
+                send("xy", r["xys"].at[sy, s], r["xyr"].at[sy, s], gy=way[sy], gx=way[s])
+                send("zy", r["zys"].at[sy, s], r["zyr"].at[sy, s], gy=way[sy], gz=way[s])
         if level == 0:
             for side in SIDES:
-                send("z", side, r["zl"].at[side], r["zr"].at[side], gz=way[side])
+                send("z", r["zl"].at[side], r["zr"].at[side], gz=way[side])
 
     def own_x(level):
         planes, tiles, height, _ = extent(level)
@@ -457,15 +461,26 @@
 
         loop(tiles * groups, 1 if level == 0 else 2, along_z)
 
-    def own_y(level, start=0, stop=None):
+    def own_y(level, start=0, stop=None, with_halos=False):
         planes, tiles, height, _ = extent(level)
         body = bodies[level]
         chunk = min(planes, 512 // height)
 
+        def halos(plane):
+            yp = held[level]["yp"]
+            window = 4 << level
+            left = pltpu.roll(yp[0, 0] + yp[1, 0], lax.rem(2 * LANES - window - plane * window, LANES), 1)
+            right = pltpu.roll(yp[0, 1] + yp[1, 1], lax.rem(LANES - plane * window, LANES), 1)
+            return jnp.where(lax.broadcasted_iota(jnp.int32, (height, LANES), 1) >= LANES // 2, left, right)
+
         def along_y(number, _):
             where = pl.ds(number * chunk, chunk)
             values = [body[where, tile].reshape(chunk * height, LANES) for tile in range(tiles)]
-            lifted = lift_lanes(values, jnp.zeros((chunk * height, LANES), f32), y_weights[level])
+            if with_halos:
+                ext = jnp.concatenate([halos(number * chunk + inner) for inner in range(chunk)], axis=0)
+            else:
+                ext = jnp.zeros((chunk * height, LANES), f32)
+            lifted = lift_lanes(values, ext, y_weights[level])
             for tile in range(tiles):
                 body[where, tile] = lifted[tile].reshape(chunk, height, LANES)
             return 0
@@ -678,7 +693,7 @@
     inner[:, 0] = inner[:, 0] + first.reshape(deep, half, LANES)
     inner[:, inner_tiles - 1] = inner[:, inner_tiles - 1] + last.reshape(deep, half, LANES)
 
-    wait_for(0, "x", "e", "c", "xy")
+    wait_for(0, "x")
     prepare_x(0)
     xl, xp = held[0]["xl"], take()
     for tile, packed in enumerate(pack_tiles(0, [xl[tile] for tile in range(tiles)])):
@@ -712,11 +727,11 @@
     own_z(1)
     own_y(1)
     own_z(0, 1)
-    own_y(0, 0, 2)
+    own_y(0, 0, 2, True)
     wait_for(1, "y")
     prepare_y(1)
     add_y(1)
-    wait_for(1, "x", "e", "c", "xy")
+    wait_for(1, "x")
     prepare_x(1)
     add_x(1)
     prepare_z(1)
@@ -738,14 +753,13 @@
     own_x(2)
     own_z(2)
     own_y(2)
-    own_y(0, 2)
-    add_y(0)
+    own_y(0, 2, None, True)
     add_x(0)
     add_z(0)
     wait_for(2, "y")
     prepare_y(2)
     add_y(2)
-    wait_for(2, "x", "e", "c", "xy")
+    wait_for(2, "x")
     prepare_x(2)
     add_x(2)
     prepare_z(2)
@@ -763,8 +777,8 @@
 
     loop(planes // 2, 4, place)
 
-    for copy in sends:
-        copy.wait_send()
+    for level in range(LEVELS):
+        wait_rows(send_sem.at[level], sent[level])
 
 
 def write_out(held_ref, inner_ref, out_ref, merged, sem):
@@ -814,8 +828,8 @@
     scratch = [vmem((planes, tiles, height, LANES), f32) for planes, tiles, height in sizes[2:]]
     scratch += [
         pltpu.SemaphoreType.DMA((3, TILES)),
-        pltpu.SemaphoreType.DMA((LEVELS, 28)),
-        pltpu.SemaphoreType.DMA((LEVELS, 28)),
+        pltpu.SemaphoreType.DMA((LEVELS,)),
+        pltpu.SemaphoreType.DMA((LEVELS, 5)),
     ]
     widths = [min(tiles, 2) * LANES for _, tiles, _ in sizes]
     scratch += [vmem((3 * (width + LANES), width), bf16) for width in widths]

time: 35.7 us -> 34.2 us (0.958)
  Pallas kernels: 35.7 us -> 34.1 us
    pallas_call x1, Pallas kernels: 33.6 us -> 32 us  [local(): pl.pallas_call(functools.partial(kernel, field.shape), out_shape=[jax.Sha...]
where the time goes in v4:
time: 34.2 us; the launch traced here: 34.1 us
  Pallas kernels  34.1 us (100%)
    pallas_call x1, Pallas kernels, local(): pl.pallas_call(functools.partial(kernel, field.shape), out_shape=[jax.Sha...  32 us
    pallas_call x1, Pallas kernels, local(): pl.pallas_call(write_out, out_shape=jax.ShapeDtypeStruct(field.shape, f32...  2.11 us

profile of v4, /device:TPU:1, one launch (start us, length us, event | category | flops | bytes accessed | tf_op | source)
XLA Modules:
  0.0 34.1 jit_solution(9162505139900638871)
XLA Ops:
  0.0 32.0 %lift.1 = (f32[32,4,64,128]{3,2,1,0:T(8,128)S(1)}, f32[16,2,32,128]{3,2,1,0:T(8,128)S(1)}) custom-call(f32[32,64,512]{2,1,0:T(8,128)} %field_ref.1), custom_call_target="tpu_custom_call" | custom-call | tf_op jit(solution)/shard_map/lift/pallas_call | solution.py:846
  32.0 2.1 %write_out.1 = f32[32,64,512]{2,1,0:T(8,128)} custom-call(f32[32,4,64,128]{3,2,1,0:T(8,128)S(1)} %get-tuple-element.7.held_ref, f32[16,2,32,128]{3,2,1,0:T(8,128)S(1)} %get-tuple-element.8.inner_ref), custom_call_target="tpu_custom_call" | custom-call | tf_op jit(solution)/shard_map/write_out/pallas_call | solution.py:857

commit v5 on v4

--- a/solution.py
+++ b/solution.py
@@ -202,13 +202,6 @@
     def beside(**by):
         return {name: near[name][way] for name, way in by.items()}
 
-    barrier = pltpu.get_barrier_semaphore()
-    for x in (-1, 0, 1):
-        for y in (-1, 0, 1):
-            for z in (-1, 0, 1):
-                if (x, y, z) != (0, 0, 0):
-                    pl.semaphore_signal(barrier, inc=1, device_id=beside(gx=x, gy=y, gz=z), device_id_type=MESH)
-
     loads = [
         [
             pltpu.make_async_copy(
@@ -220,9 +213,17 @@
         ]
         for number, (first, size) in enumerate(((0, 4), (depth - 4, 4), (4, depth - 8)))
     ]
-    for part in loads:
+    for part in loads[:2]:
         for load in part:
             load.start()
+    barrier = pltpu.get_barrier_semaphore()
+    for x in (-1, 0, 1):
+        for y in (-1, 0, 1):
+            for z in (-1, 0, 1):
+                if (x, y, z) != (0, 0, 0):
+                    pl.semaphore_signal(barrier, inc=1, device_id=beside(gx=x, gy=y, gz=z), device_id_type=MESH)
+    for load in loads[2]:
+        load.start()
 
     def fill(ref, blocks):
         start = 0
@@ -438,7 +439,7 @@
                 lift_rows(flat, (plane * tiles + tile) * height, height)
             return 0
 
-        loop(planes, 2 if level == 0 else 4, along_x)
+        loop(planes, 4, along_x)
 
     def own_z(level, parity=None):
         planes, tiles, height, _ = extent(level)
@@ -727,7 +728,7 @@
     own_z(1)
     own_y(1)
     own_z(0, 1)
-    own_y(0, 0, 2, True)
+    own_y(0, 0, 1, True)
     wait_for(1, "y")
     prepare_y(1)
     add_y(1)
@@ -753,7 +754,7 @@
     own_x(2)
     own_z(2)
     own_y(2)
-    own_y(0, 2, None, True)
+    own_y(0, 1, None, True)
     add_x(0)
     add_z(0)
     wait_for(2, "y")

time: 34.2 us -> 33.2 us (0.971)
  Pallas kernels: 34.1 us -> 33.1 us
    pallas_call x1, Pallas kernels: 32 us -> 31 us  [local(): pl.pallas_call(functools.partial(kernel, field.shape), out_shape=[jax.Sha...]
where the time goes in v5:
time: 33.2 us; the launch traced here: 33.1 us
  Pallas kernels  33.1 us (100%)
    pallas_call x1, Pallas kernels, local(): pl.pallas_call(functools.partial(kernel, field.shape), out_shape=[jax.Sha...  31 us
    pallas_call x1, Pallas kernels, local(): pl.pallas_call(write_out, out_shape=jax.ShapeDtypeStruct(field.shape, f32...  2.11 us

profile of v5, /device:TPU:1, one launch (start us, length us, event | category | flops | bytes accessed | tf_op | source)
XLA Modules:
  0.0 33.1 jit_solution(7444537214473526143)
XLA Ops:
  0.0 31.0 %lift.1 = (f32[32,4,64,128]{3,2,1,0:T(8,128)S(1)}, f32[16,2,32,128]{3,2,1,0:T(8,128)S(1)}) custom-call(f32[32,64,512]{2,1,0:T(8,128)} %field_ref.1), custom_call_target="tpu_custom_call" | custom-call | tf_op jit(solution)/shard_map/lift/pallas_call | solution.py:847
  31.0 2.1 %write_out.1 = f32[32,64,512]{2,1,0:T(8,128)} custom-call(f32[32,4,64,128]{3,2,1,0:T(8,128)S(1)} %get-tuple-element.7.held_ref, f32[16,2,32,128]{3,2,1,0:T(8,128)S(1)} %get-tuple-element.8.inner_ref), custom_call_target="tpu_custom_call" | custom-call | tf_op jit(solution)/shard_map/write_out/pallas_call | solution.py:858

commit v6 on v5

--- a/solution.py
+++ b/solution.py
@@ -462,7 +462,7 @@
 
         loop(tiles * groups, 1 if level == 0 else 2, along_z)
 
-    def own_y(level, start=0, stop=None, with_halos=False):
+    def own_y(level, start=0, stop=None):
         planes, tiles, height, _ = extent(level)
         body = bodies[level]
         chunk = min(planes, 512 // height)
@@ -477,10 +477,7 @@
         def along_y(number, _):
             where = pl.ds(number * chunk, chunk)
             values = [body[where, tile].reshape(chunk * height, LANES) for tile in range(tiles)]
-            if with_halos:
-                ext = jnp.concatenate([halos(number * chunk + inner) for inner in range(chunk)], axis=0)
-            else:
-                ext = jnp.zeros((chunk * height, LANES), f32)
+            ext = jnp.concatenate([halos(number * chunk + inner) for inner in range(chunk)], axis=0)
             lifted = lift_lanes(values, ext, y_weights[level])
             for tile in range(tiles):
                 body[where, tile] = lifted[tile].reshape(chunk, height, LANES)
@@ -610,21 +607,6 @@
                 values = jnp.where(sub == place, weights[layer], values)
         return values
 
-    def add_y(level):
-        planes, tiles, height, _ = extent(level)
-        body = bodies[level]
-        chunk = min(planes, 512 // height)
-
-        def add(number, _):
-            where = pl.ds(number * chunk, chunk)
-            added = spread_y(level, [number * chunk + inner for inner in range(chunk)], lambda ref: ref[...])
-            body[where, 0] = body[where, 0] + added[:, :LANES].reshape(chunk, height, LANES)
-            if tiles > 1:
-                body[where, tiles - 1] = body[where, tiles - 1] + added[:, LANES:].reshape(chunk, height, LANES)
-            return 0
-
-        lax.fori_loop(0, planes // chunk, add, 0)
-
     def add_x_rows(body, planes, every, height, strips, at):
         tables = ((FROM_LEFT, 0), (FROM_RIGHT, height - 8))
         weigh = [[row_weights(table, layer, at) for layer in range(2)] for table, _ in tables]
@@ -726,12 +708,11 @@
     make_weights(1)
     own_x(1)
     own_z(1)
-    own_y(1)
     own_z(0, 1)
-    own_y(0, 0, 1, True)
+    own_y(0, 0, 1)
     wait_for(1, "y")
     prepare_y(1)
-    add_y(1)
+    own_y(1)
     wait_for(1, "x")
     prepare_x(1)
     add_x(1)
@@ -753,13 +734,12 @@
     make_weights(2)
     own_x(2)
     own_z(2)
-    own_y(2)
-    own_y(0, 1, None, True)
+    own_y(0, 1)
     add_x(0)
     add_z(0)
     wait_for(2, "y")
     prepare_y(2)
-    add_y(2)
+    own_y(2)
     wait_for(2, "x")
     prepare_x(2)
     add_x(2)

time: 33.2 us -> 33.1 us (level)
  no operation moved by 1% of the time
where the time goes in v6:
time: 33.1 us; the launch traced here: 33 us
  Pallas kernels  33 us (100%)
    pallas_call x1, Pallas kernels, local(): pl.pallas_call(functools.partial(kernel, field.shape), out_shape=[jax.Sha...  30.9 us
    pallas_call x1, Pallas kernels, local(): pl.pallas_call(write_out, out_shape=jax.ShapeDtypeStruct(field.shape, f32...  2.11 us

profile of v6, /device:TPU:1, one launch (start us, length us, event | category | flops | bytes accessed | tf_op | source)
XLA Modules:
  0.0 33.0 jit_solution(7723356718263266631)
XLA Ops:
  0.0 30.9 %lift.1 = (f32[32,4,64,128]{3,2,1,0:T(8,128)S(1)}, f32[16,2,32,128]{3,2,1,0:T(8,128)S(1)}) custom-call(f32[32,64,512]{2,1,0:T(8,128)} %field_ref.1), custom_call_target="tpu_custom_call" | custom-call | tf_op jit(solution)/shard_map/lift/pallas_call | solution.py:827
  30.9 2.1 %write_out.1 = f32[32,64,512]{2,1,0:T(8,128)} custom-call(f32[32,4,64,128]{3,2,1,0:T(8,128)S(1)} %get-tuple-element.7.held_ref, f32[16,2,32,128]{3,2,1,0:T(8,128)S(1)} %get-tuple-element.8.inner_ref), custom_call_target="tpu_custom_call" | custom-call | tf_op jit(solution)/shard_map/write_out/pallas_call | solution.py:838
